TPU v7x, 1024 devices: a whole 4x4x32 slice. The times are simulated.
1024 devices in a mesh: ctx: 16 (over x, y), head: 4 (over z_hi), dp: 16 (over z_lo, core).
Axes of the slice: x: 4, y: 4, z: 32 (z_hi: 4, z_lo: 8; z = z_hi * 8 + z_lo), core: 2. Of those that a mesh axis runs over, the one named last changes fastest.
Arguments:
- query_raw: bfloat16 [16, 2048, 4096], P('dp', 'ctx', 'head'), may hold values from -6 to 6
- key_raw: bfloat16 [16, 2048, 512], P('dp', 'ctx', 'head'), may hold values from -6 to 6
- value_rows: bfloat16 [16, 2048, 512], P('dp', 'ctx', 'head'), may hold values from -6 to 6
- attn_out: bfloat16 [16, 2048, 4096], P('dp', 'ctx', 'head'), may hold values from -2 to 2
- out_grad: bfloat16 [16, 2048, 4096], P('dp', 'ctx', 'head'), may hold values from -6 to 6
- log_totals: float32 [16, 32, 2048], P('dp', 'head', 'ctx'), may hold values from -40 to 40, as said below
- query_gain: float32 [128], replicated, may hold values from 0.5 to 1.5
- key_gain: float32 [128], replicated, may hold values from 0.5 to 1.5
Outputs:
- grad_query: float32 [16, 2048, 4096], P('dp', 'ctx', 'head')
- grad_key: float32 [16, 2048, 512], P('dp', 'ctx', 'head')
- grad_value: float32 [16, 2048, 512], P('dp', 'ctx', 'head')
- gain_grads: float32 [2, 128], replicated
Inputs may be any that keep to these rules, and one draw needn't show every extreme that they name: log_totals[s, h, i] is the log of the sum over j <= i of exp(score[i, j]) for query head h, computed from query_raw, key_raw and the gains.
All inputs are finite; a program needn't handle non-finite values.
Results may differ from a plain program's by a relative error of at most 0.009.
Values may be sent and summed in bfloat16 or wider, within the bound.
No kernel may reach another device: no remote copies, remote signals or barrier semaphores. Data moves between devices by JAX's collectives and lax.ppermute only.
A program may use at most 32 MiB of HBM per device.

v0:
```python
import math

import jax
import jax.numpy as jnp
from jax import lax
from jax.sharding import PartitionSpec as P

HD = 128


def normalize(raw_rows, norm_gain):
    values = raw_rows.astype(jnp.float32).reshape(raw_rows.shape[:-1] + (-1, HD))
    inverse = lax.rsqrt(jnp.mean(values * values, axis=-1, keepdims=True) + 1e-06)
    unit_rows = values * inverse
    return (unit_rows, inverse, (unit_rows * norm_gain).astype(jnp.bfloat16))


def norm_back(grad_norm, unit_rows, inverse, norm_gain):
    grad_unit = grad_norm * norm_gain
    grad_raw = (
        grad_unit - unit_rows * jnp.mean(grad_unit * unit_rows, axis=-1, keepdims=True)
    ) * inverse
    return (grad_raw, jnp.sum(grad_norm * unit_rows, axis=(0, 1)))


def rounded_values(values):
    return lax.optimization_barrier(values.astype(jnp.bfloat16)).astype(jnp.float32)


def local(query_raw, key_raw, value_rows, attn_out, out_grad, log_totals, query_gain, key_gain):
    rows = query_raw.shape[1]
    width = query_raw.shape[2]
    kv_width = key_raw.shape[2]
    head_count = width // HD
    kv_count = kv_width // HD
    group = head_count // kv_count
    block_count = lax.axis_size("ctx")
    block_index = lax.axis_index("ctx")
    group_size = math.gcd(block_count, 4)
    step_count = block_count // group_size
    logit_scale = 1.0 / math.sqrt(HD)
    local_rows = jnp.arange(rows)
    query_list, key_list, value_list = ([], [], [])
    q_unit, q_inverse, q_norm = normalize(query_raw[0], query_gain)
    k_unit, k_inverse, k_norm = normalize(key_raw[0], key_gain)
    k_flat = k_norm.reshape(rows, kv_width)
    v_flat = value_rows[0]
    g_flat = out_grad[0]
    delta = jnp.einsum(
        "thd,thd->ht",
        g_flat.reshape(rows, head_count, HD),
        attn_out[0].reshape(rows, head_count, HD),
        preferred_element_type=jnp.float32,
    )
    delta_groups = delta.reshape(kv_count, group, rows)
    total_groups = log_totals[0].reshape(kv_count, group, rows)
    gathered = (
        lax.all_gather(k_flat, "ctx", axis=0, tiled=True),
        lax.all_gather(v_flat, "ctx", axis=0, tiled=True),
    )
    key_steps = gathered[0].reshape(step_count, group_size, rows, kv_count, HD)
    value_steps = gathered[1].reshape(step_count, group_size, rows, kv_count, HD)
    q_heads = q_norm.reshape(rows, kv_count, group, HD)
    g_heads = g_flat.reshape(rows, kv_count, group, HD)
    query_pos = block_index * rows + local_rows

    def key_step(running, inputs):
        key_group, value_group, step_index = inputs
        key_pos = step_index * group_size * rows + jnp.arange(group_size * rows).reshape(
            group_size, rows
        )
        attention_logits = (
            jnp.einsum("qcgd,pkcd->cgqpk", q_heads, key_group, preferred_element_type=jnp.float32)
            * logit_scale
        )
        causal = query_pos[:, None, None] >= key_pos[None]
        probs = jnp.where(
            causal[None, None], jnp.exp(attention_logits - total_groups[:, :, :, None, None]), 0.0
        )
        probs_low = probs.astype(jnp.bfloat16)
        value_part = jnp.einsum(
            "cgqpk,qcgd->pkcd", probs_low, g_heads, preferred_element_type=jnp.float32
        ).astype(jnp.bfloat16)
        probability_gradient = jnp.einsum(
            "qcgd,pkcd->cgqpk", g_heads, value_group, preferred_element_type=jnp.float32
        )
        score_gradient = (
            probs * (probability_gradient - delta_groups[:, :, :, None, None])
        ).astype(jnp.bfloat16)
        query_part = rounded_values(
            jnp.einsum(
                "cgqpk,pkcd->pqcgd", score_gradient, key_group, preferred_element_type=jnp.float32
            )
            * logit_scale
        )
        key_part = (
            jnp.einsum(
                "cgqpk,qcgd->pkcd", score_gradient, q_heads, preferred_element_type=jnp.float32
            )
            * logit_scale
        ).astype(jnp.bfloat16)
        return (running + jnp.sum(query_part, axis=0), (key_part, value_part))

    grad_q_groups, parts = lax.scan(
        key_step,
        jnp.zeros((rows, kv_count, group, HD), jnp.float32),
        (key_steps, value_steps, jnp.arange(step_count)),
    )
    grad_q_norm = grad_q_groups.reshape(rows, head_count, HD)
    terms = jnp.concatenate(
        [
            parts[0].reshape(block_count * rows, kv_width),
            parts[1].reshape(block_count * rows, kv_width),
        ],
        axis=1,
    )
    summed = lax.psum_scatter(
        terms.astype(jnp.float32).astype(jnp.bfloat16), "ctx", scatter_dimension=0, tiled=True
    ).astype(jnp.float32)
    grad_k_norm = summed[:, :kv_width].reshape(rows, kv_count, HD)
    grad_value = summed[:, kv_width:]
    grad_query, q_sum = norm_back(grad_q_norm, q_unit, q_inverse, query_gain)
    grad_key, k_sum = norm_back(grad_k_norm, k_unit, k_inverse, key_gain)
    query_list.append(grad_query.reshape(rows, width))
    key_list.append(grad_key.reshape(rows, kv_width))
    value_list.append(grad_value)
    summed_gains = lax.psum(jnp.stack([q_sum, k_sum]), ("ctx", "head", "dp"))
    pair_count = (
        query_raw.shape[0]
        * lax.axis_size("dp")
        * rows
        * block_count
        * head_count
        * lax.axis_size("head")
    )
    gain_grads = summed_gains * (1.0 / math.sqrt(pair_count))
    return (jnp.stack(query_list), jnp.stack(key_list), jnp.stack(value_list), gain_grads)


def solution(mesh):
    return jax.shard_map(
        local,
        mesh=mesh,
        in_specs=(
            P("dp", "ctx", "head"),
            P("dp", "ctx", "head"),
            P("dp", "ctx", "head"),
            P("dp", "ctx", "head"),
            P("dp", "ctx", "head"),
            P("dp", "head", "ctx"),
            P(),
            P(),
        ),
        out_specs=(P("dp", "ctx", "head"), P("dp", "ctx", "head"), P("dp", "ctx", "head"), P()),
        check_vma=False,
    )
```

profile of v0, /device:TPU:1, one launch (start us, length us, event | category | flops | bytes accessed | tf_op | source)
XLA Modules:
  0.0 365.2 jit_solution(5341087135213494047)
XLA Ops:
  7.3 0.9 fusion.50
  8.2 1.0 copy.90
  9.2 1.1 copy.62
  10.3 1.0 copy.89
  11.3 0.2 fusion.36
  11.6 0.2 copy.64
  11.9 20.0 %all_gather.6 = bf16[2048,128]{1,0:T(8,128)(2,1)S(1)} all-gather(bf16[128,128]{1,0:T(8,128)(2,1)S(1)} %fusion.44), channel_id=1, replica_groups=mesh['ctx'=16,'head'=4,'dp'=16] {'ctx'}, dimensions={0}, use_global_device_ids=true | all-gather | bytes 557056 | tf_op jit(solution)/shard_map/all_gather | solution.py:58
  31.9 18.6 %all-gather = bf16[1,2048,128]{2,1,0:T(8,128)(2,1)S(1)} all-gather(bf16[1,128,128]{2,1,0:T(8,128)(2,1)S(1)} %copy-done.2), channel_id=2, replica_groups=mesh['ctx'=16,'head'=4,'dp'=16] {'ctx'}, dimensions={1}, use_global_device_ids=true | all-gather | bytes 557056 | tf_op jit(solution)/shard_map/all_gather | solution.py:59
  50.7 0.2 multiply_reduce_fusion
  50.9 0.2 fusion.38
  51.2 19.5 %while.17 = (s32[]{:T(128)}, f32[128,1,8,128]{0,3,2,1:T(8,128)S(1)}, bf16[4,4,128,1,128]{4,2,1,3,0:T(8,128)(2,1)}, bf16[4,4,128,1,128]{4,2,1,3,0:T(8,128)(2,1)S(...) while((s32[]{:T(128)}, ...), condition=%wide.region_4.5_spmd.clone, body=%wide.region_2.4_spmd.clone.sunk | while | flops 677250688 | bytes 15480019 | solution.py:104
  51.2 0.6 dynamic_slice.42
  52.6 0.6 fusion.78
  53.2 0.5 fusion.82
  53.7 0.4 fusion.79
  54.1 1.1 fusion.81
  55.2 0.5 fusion.80
  55.9 0.2 bitcast_add_fusion.2
  56.1 0.6 dynamic_slice.42
  57.5 0.6 fusion.78
  58.1 0.5 fusion.82
  58.6 0.4 fusion.79
  59.0 1.1 fusion.81
  60.1 0.5 fusion.80
  61.0 0.6 dynamic_slice.42
  62.4 0.6 fusion.78
  62.9 0.5 fusion.82
  63.4 0.4 fusion.79
  63.9 1.1 fusion.81
  65.0 0.5 fusion.80
  65.8 0.6 dynamic_slice.42
  67.2 0.6 fusion.78
  67.8 0.5 fusion.82
  68.3 0.4 fusion.79
  68.8 1.1 fusion.81
  69.9 0.5 fusion.80
  70.7 2.1 pad_maximum_fusion
  72.9 0.2 copy.67
  73.2 0.2 copy.84
  73.6 0.2 mul.234
  73.9 0.2 copy.83
  74.1 0.9 fusion.32
  75.1 120.9 %reduce-scatter.2.cloned.1.call-done = bf16[128,256]{1,0:T(8,128)(2,1)} async-done(((bf16[2048,256]{1,0:T(8,128)(2,1)}), bf16[128,256]{1,0:T(8,128)(2,1)}) %reduce-scatter.2.cloned.1.call-update) | async-done | bytes 65552 | tf_op jit(solution)/shard_map/reduce_scatter | solution.py:117
  195.9 0.8 convert_element_type.135
  196.8 0.7 fusion.49
  197.5 159.5 %psum.7 = f32[2,128]{1,0:T(2,128)S(1)} all-reduce(f32[2,128]{1,0:T(2,128)S(1)} %pad_maximum_fusion.1), channel_id=1, replica_groups=mesh['ctx'=16,'head'=4,'dp'=16] {'ctx','head','dp'}, use_global_device_ids=true, to_apply=%region_10.11 | all-reduce | flops 256 | bytes 2048 | tf_op jit(solution)/shard_map/psum | solution.py:127
  357.0 0.6 broadcast_multiply_fusion.1
  357.6 0.7 fusion.48
  (52 shorter events, 2.6 us)
Async XLA Ops:
  7.2 4.6 %copy-start.1 = (bf16[1,128,128]{2,1,0:T(8,128)(2,1)S(1)}, bf16[1,128,128]{2,1,0:T(8,128)(2,1)}, u32[]{:S(2)}) copy-start(bf16[1,128,128]{2,1,0:T(8,128)(2,1)} %param.11) | copy-start | bytes 98308
  7.2 4.6 %copy-start.4 = (f32[128]{0:T(128)S(1)}, f32[128]{0:T(128)}, u32[]{:S(2)}) copy-start(f32[128]{0:T(128)} %param.17) | copy-start | bytes 1540
  7.2 24.7 %copy-start.2 = (bf16[1,128,128]{2,1,0:T(8,128)(2,1)S(1)}, bf16[1,128,128]{2,1,0:T(8,128)(2,1)}, u32[]{:S(2)}) copy-start(bf16[1,128,128]{2,1,0:T(8,128)(2,1)} %param.12) | copy-start | bytes 98308
  7.2 43.3 %copy-start = (bf16[1,128,1024]{2,1,0:T(8,128)(2,1)S(1)}, bf16[1,128,1024]{2,1,0:T(8,128)(2,1)}, u32[]{:S(2)}) copy-start(bf16[1,128,1024]{2,1,0:T(8,128)(2,1)} %param.10) | copy-start | bytes 786436
  7.2 188.7 %reduce-scatter.2.cloned.1.call-start = ((), (), s32[]{:S(2)}) async-start(), calls=%async_computation.1 | async-start | bytes 1114112 | tf_op jit(solution)/shard_map/reduce_scatter | solution.py:117
  11.6 39.3 %copy-start.3 = (f32[128]{0:T(128)S(1)}, f32[128]{0:T(128)}, u32[]{:S(2)}) copy-start(f32[128]{0:T(128)} %param.16) | copy-start | bytes 1540
  11.9 39.3 %copy-start.5 = (f32[1,8,128]{2,1,0:T(8,128)S(1)}, f32[1,8,128]{2,1,0:T(8,128)}, u32[]{:S(2)}) copy-start(f32[1,8,128]{2,1,0:T(8,128)} %param.15) | copy-start | bytes 12292
Sparse Core Ops, SparseCore 0:
  73.0 122.8 reduce-scatter.1
where the time goes:
time: 366 us; the launch traced here: 365 us
  blocking collectives  198 us (54%)
  waiting for transfers between devices  121 us (33%)
  between operations  14.3 us (4%)
  matrix products  12.4 us (3%)
  other arithmetic  9.72 us (3%)
  local copies, waits for them, and re-layouts  6.92 us (2%)
    psum x1, blocking collectives, local(): summed_gains = lax.psum(jnp.stack([q_sum, k_sum]), ('ctx', 'head', 'dp'))  160 us
    reduce_scatter x1, waiting for transfers between devices, local(): lax.psum_scatter(terms.astype(jnp.float32).astype(jnp.bfloat16), 'ctx', s...  121 us
    all_gather x1, blocking collectives, local(): lax.all_gather(k_flat, 'ctx', axis=0, tiled=True)  20 us
    all_gather x1, blocking collectives, local(): lax.all_gather(v_flat, 'ctx', axis=0, tiled=True)  18.6 us
  transfers between devices with their start and end apart: 1, of which 1 were waited for; matrix products, arithmetic and copies ran while one was open for 1% of the time, Pallas kernels for 0%

commit v1 on v0

v1 whole, which is shorter than its diff:
```python
import functools
import math

import jax
import jax.numpy as jnp
from jax import lax
from jax.experimental import pallas as pl
from jax.experimental.pallas import tpu as pltpu
from jax.sharding import PartitionSpec as P

HD = 128
TAIL = 8
EPS = 1e-06
LOG2E = 1.4426950408889634
F32 = jnp.float32
BF16 = jnp.bfloat16


def prologue(q_ref, o_ref, g_ref, lt_ref, qgain_ref, qn_ref, qt_ref, ut_ref, gs_ref, gt_ref, rows_ref):
    rows = q_ref.shape[0]
    for h in range(q_ref.shape[1] // HD):
        cols = slice(h * HD, (h + 1) * HD)
        span = slice(h * rows, (h + 1) * rows)
        q = q_ref[:, cols].astype(F32)
        inverse = lax.rsqrt(jnp.mean(q * q, axis=-1, keepdims=True) + EPS)
        unit = q * inverse
        ut_ref[:, span] = unit.T
        qn = (unit * qgain_ref[...]).astype(BF16)
        qn_ref[span, :] = qn
        qt_ref[:, span] = qn.astype(F32).T.astype(BF16)
        g = g_ref[:, cols]
        gs_ref[span, :] = g
        g_turned = g.astype(F32).T
        gt_ref[:, span] = g_turned.astype(BF16)
        o_turned = o_ref[:, cols].astype(F32).T
        rows_ref[0:1, span] = lt_ref[h : h + 1, :] * LOG2E
        rows_ref[1:2, span] = jnp.sum(g_turned * o_turned, axis=0, keepdims=True)


def attention(
    block_ref, kv_ref, qn_ref, qt_ref, ut_ref, gs_ref, gt_ref, rows_ref, kgain_ref,
    dqt_ref, parts_ref,
    kn_ref, kt_ref, unit_ref,
):
    blocks, rows = kv_ref.shape[0], kv_ref.shape[1]
    width = qt_ref.shape[1]
    scale = 1.0 / math.sqrt(HD)
    pair = 2 * rows
    wide = 2 * rows
    block = block_ref[0]
    last = block // 2
    for j in range(blocks // 2):
        k = kv_ref[2 * j : 2 * j + 2, :, :HD].reshape(pair, HD).astype(F32)
        inverse = lax.rsqrt(jnp.mean(k * k, axis=-1, keepdims=True) + EPS)
        unit = k * inverse
        kn = (unit * kgain_ref[...]).astype(BF16)
        unit_ref[j] = unit
        kn_ref[j] = kn
        kt_ref[j] = kn.astype(F32).T.astype(BF16)
    dqt_ref[...] = jnp.zeros(dqt_ref.shape, F32)

    def step(j, k_gain, masked):
        kn = kn_ref[j]
        kt = kt_ref[j]
        v = kv_ref[pl.ds(2 * j, 2), :, HD:].reshape(pair, HD)
        dk = jnp.zeros((pair, HD), F32)
        dv = jnp.zeros((pair, HD), F32)
        if masked:
            key_pos = j * pair + lax.broadcasted_iota(jnp.int32, (pair, wide), 0)
            query_pos = block * rows + lax.broadcasted_iota(jnp.int32, (pair, wide), 1) % rows
            keep = key_pos <= query_pos
        for c in range(width // wide):
            span = slice(c * wide, (c + 1) * wide)
            scores = jnp.dot(kn, qt_ref[:, span], preferred_element_type=F32)
            probs = jnp.exp2(scores * (scale * LOG2E) - rows_ref[0:1, span])
            if masked:
                probs = jnp.where(keep, probs, 0.0)
            dv += jnp.dot(probs.astype(BF16), gs_ref[span, :], preferred_element_type=F32)
            dp = jnp.dot(v, gt_ref[:, span], preferred_element_type=F32)
            ds = (probs * (dp - rows_ref[1:2, span])).astype(BF16)
            dk += jnp.dot(ds, qn_ref[span, :], preferred_element_type=F32)
            dqt_ref[:, span] += jnp.dot(kt, ds, preferred_element_type=F32)
        dk = dk * scale
        parts_ref[pl.ds(2 * j, 2), :rows, :HD] = dk.astype(BF16).reshape(2, rows, HD)
        parts_ref[pl.ds(2 * j, 2), :rows, HD:] = dv.astype(BF16).reshape(2, rows, HD)
        return k_gain + jnp.sum(dk * unit_ref[j], axis=0, keepdims=True)

    k_gain = lax.fori_loop(0, last, lambda j, s: step(j, s, False), jnp.zeros((1, HD), F32))
    k_gain = step(last, k_gain, True)

    def clear(j, carry):
        parts_ref[pl.ds(2 * j, 2), :rows] = jnp.zeros((2, rows, 2 * HD), BF16)
        return carry

    lax.fori_loop(last + 1, blocks // 2, clear, 0)
    product = jnp.zeros((HD, wide), F32)
    for c in range(width // wide):
        span = slice(c * wide, (c + 1) * wide)
        product += dqt_ref[:, span] * ut_ref[:, span]
    q_gain = jnp.sum((product[:, :HD] + product[:, HD:]).T, axis=0, keepdims=True) * scale
    sums = jnp.concatenate([q_gain, k_gain], axis=1)
    high = sums.astype(BF16).astype(F32)
    middle = (sums - high).astype(BF16).astype(F32)
    low = sums - high - middle
    tail = jnp.concatenate([high, middle, low, jnp.zeros((TAIL - 3, 2 * HD), F32)], axis=0)
    tail = tail.astype(BF16)
    for b in range(blocks):
        parts_ref[b, rows:] = tail


def query_end(dqt_ref, q_ref, qgain_ref, gq_ref):
    rows = q_ref.shape[0]
    scale = 1.0 / math.sqrt(HD)
    for h in range(q_ref.shape[1] // HD):
        cols = slice(h * HD, (h + 1) * HD)
        grad_norm = dqt_ref[:, h * rows : (h + 1) * rows].T * scale
        q = q_ref[:, cols].astype(F32)
        inverse = lax.rsqrt(jnp.mean(q * q, axis=-1, keepdims=True) + EPS)
        unit = q * inverse
        grad_unit = grad_norm * qgain_ref[...]
        mean = jnp.mean(grad_unit * unit, axis=-1, keepdims=True)
        gq_ref[:, cols] = (grad_unit - unit * mean) * inverse


def near_sum(parts_ref, gains_ref):
    total = parts_ref[0, -TAIL:].astype(F32)
    for b in range(1, parts_ref.shape[0]):
        total += parts_ref[b, -TAIL:].astype(F32)
    sums = jnp.sum(total, axis=0, keepdims=True)
    sums = jnp.concatenate([sums[:, :HD], sums[:, HD:]], axis=0)
    for i in range(gains_ref.shape[0]):
        gains_ref[i] = sums


def far_sum(gains_ref, out_ref, *, factor):
    out_ref[...] = jnp.sum(gains_ref[...], axis=0) * factor


def key_end(parts_ref, k_ref, kgain_ref, gk_ref, gv_ref):
    rows = k_ref.shape[0]
    total = parts_ref[0, :rows].astype(F32)
    for b in range(1, parts_ref.shape[0]):
        total += parts_ref[b, :rows].astype(F32)
    grad_norm = total[:, :HD]
    gv_ref[...] = total[:, HD:]
    k = k_ref[...].astype(F32)
    inverse = lax.rsqrt(jnp.mean(k * k, axis=-1, keepdims=True) + EPS)
    unit = k * inverse
    grad_unit = grad_norm * kgain_ref[...]
    mean = jnp.mean(grad_unit * unit, axis=-1, keepdims=True)
    gk_ref[...] = (grad_unit - unit * mean) * inverse


def spread_rows(k_ref, v_ref, out_ref):
    both = jnp.concatenate([k_ref[...], v_ref[...]], axis=1)
    for b in range(out_ref.shape[0]):
        out_ref[b] = both


def local(query_raw, key_raw, value_rows, attn_out, out_grad, log_totals, query_gain, key_gain):
    blocks = lax.axis_size("ctx")
    rows, width = query_raw.shape[1], query_raw.shape[2]
    heads = width // HD
    others = lax.axis_size("head") * lax.axis_size("dp")
    shape = jax.ShapeDtypeStruct
    query_gain = query_gain.reshape(1, HD)
    key_gain = key_gain.reshape(1, HD)
    spread = pl.pallas_call(
        spread_rows, out_shape=shape((blocks, rows, 2 * HD), BF16), name="spread_rows"
    )(key_raw[0], value_rows[0])
    gathered = lax.all_to_all(spread, "ctx", 0, 0, tiled=True)
    prepared = pl.pallas_call(
        prologue,
        out_shape=(
            shape((heads * rows, HD), BF16),
            shape((HD, heads * rows), BF16),
            shape((HD, heads * rows), F32),
            shape((heads * rows, HD), BF16),
            shape((HD, heads * rows), BF16),
            shape((2, heads * rows), F32),
        ),
        name="prologue",
    )(query_raw[0], attn_out[0], out_grad[0], log_totals[0], query_gain)
    in_vmem = pl.BlockSpec(memory_space=pltpu.VMEM)
    dqt, parts = pl.pallas_call(
        attention,
        out_shape=(shape((HD, heads * rows), F32), shape((blocks, rows + TAIL, 2 * HD), BF16)),
        in_specs=[pl.BlockSpec(memory_space=pltpu.SMEM)] + [in_vmem] * 8,
        scratch_shapes=[
            pltpu.VMEM((blocks // 2, 2 * rows, HD), BF16),
            pltpu.VMEM((blocks // 2, HD, 2 * rows), BF16),
            pltpu.VMEM((blocks // 2, 2 * rows, HD), F32),
        ],
        name="attention",
    )(lax.axis_index("ctx").reshape(1).astype(jnp.int32), gathered, *prepared, key_gain)
    returned = lax.all_to_all(parts, "ctx", 0, 0, tiled=True)
    grad_query = pl.pallas_call(
        query_end, out_shape=shape((rows, width), F32), name="query_end"
    )(dqt, query_raw[0], query_gain)
    gains = pl.pallas_call(
        near_sum, out_shape=shape((others, 2, HD), F32), name="near_sum"
    )(returned)
    gains = lax.all_to_all(gains, ("head", "dp"), 0, 0, tiled=True)
    grad_key, grad_value = pl.pallas_call(
        key_end,
        out_shape=(shape((rows, HD), F32), shape((rows, HD), F32)),
        name="key_end",
    )(returned, key_raw[0], key_gain)
    pair_count = query_raw.shape[0] * rows * blocks * heads * others
    gains = pl.pallas_call(
        functools.partial(far_sum, factor=1.0 / math.sqrt(pair_count)),
        out_shape=shape((2, HD), F32),
        name="far_sum",
    )(gains)
    return (grad_query[None], grad_key[None], grad_value[None], gains)


def solution(mesh):
    return jax.shard_map(
        local,
        mesh=mesh,
        in_specs=(
            P("dp", "ctx", "head"),
            P("dp", "ctx", "head"),
            P("dp", "ctx", "head"),
            P("dp", "ctx", "head"),
            P("dp", "ctx", "head"),
            P("dp", "head", "ctx"),
            P(),
            P(),
        ),
        out_specs=(P("dp", "ctx", "head"), P("dp", "ctx", "head"), P("dp", "ctx", "head"), P()),
        check_vma=False,
    )
```

time: 366 us -> 120 us (0.33)
  blocking collectives: 198 us -> 22.7 us
  waiting for transfers between devices: 121 us -> 29.2 us
  starting transfers between devices: 0.04 us -> 48 us
  Pallas kernels: 0 us -> 17.6 us
  between operations: 14.3 us -> 0.66 us
  matrix products: 12.4 us -> 0 us
  other arithmetic: 9.72 us -> 0 us
  local copies, waits for them, and re-layouts: 6.92 us -> 1.61 us
    psum x1 -> x0, blocking collectives: 160 us -> none  [local(): summed_gains = lax.psum(jnp.stack([q_sum, k_sum]), ('ctx', 'head', 'dp'))]
    reduce_scatter x1 -> x0, waiting for transfers between devices: 121 us -> none  [local(): lax.psum_scatter(terms.astype(jnp.float32).astype(jnp.bfloat16), 'ctx', s...]
    all_to_all x0 -> x2, starting transfers between devices: none -> 48 us  [the longest x1 40.4 us: local(): gains = lax.all_to_all(gains, ('head', 'dp'), 0, 0, tiled=True)]
    all_gather x2 -> x0, blocking collectives: 38.6 us -> none  [the longest x1 20 us: local(): lax.all_gather(k_flat, 'ctx', axis=0, tiled=True)]
    all_to_all x0 -> x2, waiting for transfers between devices: none -> 29.2 us  [the longest x1 20.1 us: local(): gains = lax.all_to_all(gains, ('head', 'dp'), 0, 0, tiled=True)]
    all_to_all x0 -> x1, blocking collectives: none -> 22.7 us  [local(): returned = lax.all_to_all(parts, 'ctx', 0, 0, tiled=True)]
    pallas_call x0 -> x7, Pallas kernels: none -> 17.6 us  [the longest x1 4.67 us: local(): pl.pallas_call(attention, out_shape=(shape((HD, heads * rows), F32), shap...]
    dot_general x20 -> x0, matrix products: 12.4 us -> none  [the longest x4 4.41 us: key_step(): jnp.einsum('cgqpk,qcgd->pkcd', score_gradient, q_heads, preferred_element...]
  transfers between devices with their start and end apart: 1 -> 2, of which waited for: 1 -> 2; matrix products, arithmetic and copies ran while one was open for 1% -> 0% of each run, Pallas kernels for 0% -> 6%
where the time goes in v1:
time: 120 us
  starting transfers between devices  48 us (40%)
  waiting for transfers between devices  29.2 us (24%)
  blocking collectives  22.7 us (19%)
  Pallas kernels  17.6 us (15%)
  local copies, waits for them, and re-layouts  1.61 us (1%)
    all_to_all x1, starting transfers between devices, local(): gains = lax.all_to_all(gains, ('head', 'dp'), 0, 0, tiled=True)  40.4 us
    all_to_all x1, blocking collectives, local(): returned = lax.all_to_all(parts, 'ctx', 0, 0, tiled=True)  22.7 us
    all_to_all x1, waiting for transfers between devices, local(): gains = lax.all_to_all(gains, ('head', 'dp'), 0, 0, tiled=True)  20.1 us
    all_to_all x1, waiting for transfers between devices, local(): gathered = lax.all_to_all(spread, 'ctx', 0, 0, tiled=True)  9.04 us
    all_to_all x1, starting transfers between devices, local(): gathered = lax.all_to_all(spread, 'ctx', 0, 0, tiled=True)  7.57 us
    pallas_call x1, Pallas kernels, local(): pl.pallas_call(attention, out_shape=(shape((HD, heads * rows), F32), shap...  4.67 us
    pallas_call x1, Pallas kernels, local(): pl.pallas_call(query_end, out_shape=shape((rows, width), F32), name='quer...  2.89 us
    pallas_call x1, Pallas kernels, local(): pl.pallas_call(prologue, out_shape=(shape((heads * rows, HD), BF16), shap...  2.71 us
  transfers between devices with their start and end apart: 2, of which 2 were waited for; matrix products, arithmetic and copies ran while one was open for 0% of the time, Pallas kernels for 6%

profile of v1, /device:TPU:1, one launch (start us, length us, event | category | flops | bytes accessed | tf_op | source)
XLA Modules:
  0.0 119.7 jit_solution(16088985963601279648)
XLA Ops:
  0.6 1.8 %spread_rows.1 = bf16[16,128,256]{2,1,0:T(8,128)(2,1)} custom-call(bf16[128,128]{1,0:T(8,128)(2,1)} %bitcast.17, bf16[128,128]{1,0:T(8,128)(2,1)} %bitcast.19), custom_call_target="tpu_custom_call" | custom-call | tf_op jit(solution)/shard_map/spread_rows/pallas_call | solution.py:168
  2.5 7.6 %all-to-all-start = ((bf16[16,128,256]{2,1,0:T(8,128)(2,1)}), bf16[16,128,256]{2,1,0:T(8,128)(2,1)S(1)}, u32[]{:S(2)}, u32[]{:S(2)}) async-start(bf16[16,128,256]{2,1,0:T(8,128)(2,1)} %spread_rows.1), calls=%async_computation | async-start | bytes 2097152 | tf_op jit(solution)/shard_map/all_to_all | solution.py:171
  10.1 2.7 %prologue.1 = (bf16[1024,128]{1,0:T(8,128)(2,1)}, bf16[128,1024]{1,0:T(8,128)(2,1)}, f32[128,1024]{1,0:T(8,128)}, bf16[1024,128]{1,0:T(8,128)(2,1)}, bf16[128,1024]{1,0:T(8,128)(2,1)}, /*index=5*/f32[2,1024]{1,0:T(2,128)}) custom-call(bf16[128,1024]{1,0:T(8,128)(2,1)} %bitcast.12, bf16[128,1024]{1,0:T(8,128)(2,1)} %bitcast.15, bf16[128,1024]{1,0:T(8,128)(2,1)} %bitcast.16, ...), custom_call_target="tpu_custom_call" | custom-call | tf_op jit(solution)/shard_map/prologue/pallas_call | solution.py:172
  12.8 9.0 %all-to-all-done.kv_ref = bf16[16,128,256]{2,1,0:T(8,128)(2,1)S(1)} async-done(((bf16[16,128,256]{2,1,0:T(8,128)(2,1)}), bf16[16,128,256]{2,1,0:T(8,128)(2,1)S(1)}, u32[]{:S(2)}, u32[]{:S(2)}) %all-to-all-start) | async-done | bytes 1048608 | tf_op jit(solution)/shard_map/all_to_all | solution.py:171
  21.8 0.0 copy-start
  21.8 1.0 copy-done
  22.8 4.7 %attention.1 = (f32[128,1024]{1,0:T(8,128)}, bf16[16,136,256]{2,1,0:T(8,128)(2,1)}) custom-call(s32[1]{0:T(128)} %bitcast.block_ref, bf16[16,128,256]{2,1,0:T(8,128)(2,1)} %copy-done, bf16[1024,128]{1,0:T(8,128)(2,1)} %get-tuple-element.14.qn_ref, bf16[128,1024]{1,0:T(8,128)(2,1)} %get-tuple-element.15.qt_ref, f32[128,1024]{1,0:T(8,128)} %get-tuple-element.16.ut_ref, ...), custom_call_target="tpu_custom_call" | custom-call | tf_op jit(solution)/shard_map/attention/pallas_call | solution.py:185
  27.5 22.7 %all_to_all.15.parts_ref = bf16[16,136,256]{2,1,0:T(8,128)(2,1)} all-to-all(bf16[16,136,256]{2,1,0:T(8,128)(2,1)} %get-tuple-element.21), channel_id=1, replica_groups=mesh['ctx'=16,'head'=4,'dp'=16] {'ctx'}, dimensions={0} | all-to-all | bytes 2228224 | tf_op jit(solution)/shard_map/all_to_all | solution.py:196
  50.2 1.9 %near_sum.1 = f32[64,2,128]{2,1,0:T(2,128)} custom-call(bf16[16,136,256]{2,1,0:T(8,128)(2,1)} %all_to_all.15.parts_ref), custom_call_target="tpu_custom_call" | custom-call | tf_op jit(solution)/shard_map/near_sum/pallas_call | solution.py:200
  52.1 40.4 %all-to-all-start.2 = ((f32[64,2,128]{2,1,0:T(2,128)}), f32[64,2,128]{2,1,0:T(2,128)S(1)}, u32[]{:S(2)}, u32[]{:S(2)}) async-start(f32[64,2,128]{2,1,0:T(2,128)} %near_sum.1), calls=%async_computation.2 | async-start | bytes 131072 | tf_op jit(solution)/shard_map/all_to_all | solution.py:203
  92.5 2.9 %query_end.1 = f32[128,1024]{1,0:T(8,128)} custom-call(f32[128,1024]{1,0:T(8,128)} %get-tuple-element.20.dqt_ref, bf16[128,1024]{1,0:T(8,128)(2,1)} %bitcast.13, f32[1,128]{1,0:T(1,128)} %bitcast.24), custom_call_target="tpu_custom_call" | custom-call | tf_op jit(solution)/shard_map/query_end/pallas_call | solution.py:197
  95.4 2.1 %key_end.1 = (f32[128,128]{1,0:T(8,128)}, f32[128,128]{1,0:T(8,128)}) custom-call(bf16[16,136,256]{2,1,0:T(8,128)(2,1)} %all_to_all.15.parts_ref, bf16[128,128]{1,0:T(8,128)(2,1)} %bitcast.18, f32[1,128]{1,0:T(1,128)} %bitcast.22), custom_call_target="tpu_custom_call" | custom-call | tf_op jit(solution)/shard_map/key_end/pallas_call | solution.py:204
  97.5 20.1 %all-to-all-done.2.gains_ref = f32[64,2,128]{2,1,0:T(2,128)S(1)} async-done(((f32[64,2,128]{2,1,0:T(2,128)}), f32[64,2,128]{2,1,0:T(2,128)S(1)}, u32[]{:S(2)}, u32[]{:S(2)}) %all-to-all-start.2) | async-done | bytes 65568 | tf_op jit(solution)/shard_map/all_to_all | solution.py:203
  117.6 0.0 copy-start.1
  117.6 0.6 copy-done.1
  118.3 1.5 %far_sum.1 = f32[2,128]{1,0:T(2,128)} custom-call(f32[64,2,128]{2,1,0:T(2,128)} %copy-done.1), custom_call_target="tpu_custom_call" | custom-call | tf_op jit(solution)/shard_map/far_sum/pallas_call | solution.py:210
Async XLA Ops:
  2.5 19.3 %all-to-all-start = ((bf16[16,128,256]{2,1,0:T(8,128)(2,1)}), bf16[16,128,256]{2,1,0:T(8,128)(2,1)S(1)}, u32[]{:S(2)}, u32[]{:S(2)}) async-start(bf16[16,128,256]{2,1,0:T(8,128)(2,1)} %spread_rows.1), calls=%async_computation | async-start | bytes 2097152 | tf_op jit(solution)/shard_map/all_to_all | solution.py:171
  21.8 1.0 copy-start
  52.1 65.6 %all-to-all-start.2 = ((f32[64,2,128]{2,1,0:T(2,128)}), f32[64,2,128]{2,1,0:T(2,128)S(1)}, u32[]{:S(2)}, u32[]{:S(2)}) async-start(f32[64,2,128]{2,1,0:T(2,128)} %near_sum.1), calls=%async_computation.2 | async-start | bytes 131072 | tf_op jit(solution)/shard_map/all_to_all | solution.py:203
  117.6 0.6 copy-start.1

commit v2 on v1

--- a/solution.py
+++ b/solution.py
@@ -10,6 +10,9 @@
 
 HD = 128
 TAIL = 8
+VMEM_LIMIT = 32 * 2**20
+CTX_FIRST = 10
+FAR_FIRST = 40
 EPS = 1e-06
 LOG2E = 1.4426950408889634
 F32 = jnp.float32
@@ -49,6 +52,7 @@
     wide = 2 * rows
     block = block_ref[0]
     last = block // 2
+    turn = blocks // 2 - CTX_FIRST % blocks // 2
     for j in range(blocks // 2):
         k = kv_ref[2 * j : 2 * j + 2, :, :HD].reshape(pair, HD).astype(F32)
         inverse = lax.rsqrt(jnp.mean(k * k, axis=-1, keepdims=True) + EPS)
@@ -60,9 +64,10 @@
     dqt_ref[...] = jnp.zeros(dqt_ref.shape, F32)
 
     def step(j, k_gain, masked):
-        kn = kn_ref[j]
-        kt = kt_ref[j]
-        v = kv_ref[pl.ds(2 * j, 2), :, HD:].reshape(pair, HD)
+        at = (j + turn) % (blocks // 2)
+        kn = kn_ref[at]
+        kt = kt_ref[at]
+        v = kv_ref[pl.ds(2 * at, 2), :, HD:].reshape(pair, HD)
         dk = jnp.zeros((pair, HD), F32)
         dv = jnp.zeros((pair, HD), F32)
         if masked:
@@ -81,15 +86,16 @@
             dk += jnp.dot(ds, qn_ref[span, :], preferred_element_type=F32)
             dqt_ref[:, span] += jnp.dot(kt, ds, preferred_element_type=F32)
         dk = dk * scale
-        parts_ref[pl.ds(2 * j, 2), :rows, :HD] = dk.astype(BF16).reshape(2, rows, HD)
-        parts_ref[pl.ds(2 * j, 2), :rows, HD:] = dv.astype(BF16).reshape(2, rows, HD)
-        return k_gain + jnp.sum(dk * unit_ref[j], axis=0, keepdims=True)
+        parts_ref[pl.ds(2 * at, 2), :rows, :HD] = dk.astype(BF16).reshape(2, rows, HD)
+        parts_ref[pl.ds(2 * at, 2), :rows, HD:] = dv.astype(BF16).reshape(2, rows, HD)
+        return k_gain + jnp.sum(dk * unit_ref[at], axis=0, keepdims=True)
 
     k_gain = lax.fori_loop(0, last, lambda j, s: step(j, s, False), jnp.zeros((1, HD), F32))
     k_gain = step(last, k_gain, True)
 
     def clear(j, carry):
-        parts_ref[pl.ds(2 * j, 2), :rows] = jnp.zeros((2, rows, 2 * HD), BF16)
+        at = (j + turn) % (blocks // 2)
+        parts_ref[pl.ds(2 * at, 2), :rows] = jnp.zeros((2, rows, 2 * HD), BF16)
         return carry
 
     lax.fori_loop(last + 1, blocks // 2, clear, 0)
@@ -127,13 +133,13 @@
     for b in range(1, parts_ref.shape[0]):
         total += parts_ref[b, -TAIL:].astype(F32)
     sums = jnp.sum(total, axis=0, keepdims=True)
-    sums = jnp.concatenate([sums[:, :HD], sums[:, HD:]], axis=0)
+    sums = jnp.concatenate([sums[:, :HD], sums[:, HD:]], axis=0).astype(BF16)
     for i in range(gains_ref.shape[0]):
         gains_ref[i] = sums
 
 
 def far_sum(gains_ref, out_ref, *, factor):
-    out_ref[...] = jnp.sum(gains_ref[...], axis=0) * factor
+    out_ref[...] = jnp.sum(gains_ref[...].astype(F32), axis=0) * factor
 
 
 def key_end(parts_ref, k_ref, kgain_ref, gk_ref, gv_ref):
@@ -157,61 +163,75 @@
         out_ref[b] = both
 
 
+def local_memory(values):
+    return pltpu.with_memory_space_constraint(values, pltpu.VMEM)
+
+
+def exchange(values, axes, count, first):
+    order = [[(first + i) % count for i in range(count)]]
+    return lax.all_to_all(values, axes, 0, 0, axis_index_groups=order, tiled=True)
+
+
 def local(query_raw, key_raw, value_rows, attn_out, out_grad, log_totals, query_gain, key_gain):
     blocks = lax.axis_size("ctx")
     rows, width = query_raw.shape[1], query_raw.shape[2]
     heads = width // HD
     others = lax.axis_size("head") * lax.axis_size("dp")
     shape = jax.ShapeDtypeStruct
+    near = pltpu.VMEM
+    params = pltpu.CompilerParams(vmem_limit_bytes=VMEM_LIMIT)
+    in_vmem = pl.BlockSpec(memory_space=pltpu.VMEM)
     query_gain = query_gain.reshape(1, HD)
     key_gain = key_gain.reshape(1, HD)
     spread = pl.pallas_call(
-        spread_rows, out_shape=shape((blocks, rows, 2 * HD), BF16), name="spread_rows"
+        spread_rows, out_shape=near((blocks, rows, 2 * HD), BF16), name="spread_rows", compiler_params=params
     )(key_raw[0], value_rows[0])
-    gathered = lax.all_to_all(spread, "ctx", 0, 0, tiled=True)
+    gathered = exchange(spread, "ctx", blocks, CTX_FIRST)
     prepared = pl.pallas_call(
         prologue,
         out_shape=(
-            shape((heads * rows, HD), BF16),
-            shape((HD, heads * rows), BF16),
-            shape((HD, heads * rows), F32),
-            shape((heads * rows, HD), BF16),
-            shape((HD, heads * rows), BF16),
-            shape((2, heads * rows), F32),
+            near((heads * rows, HD), BF16),
+            near((HD, heads * rows), BF16),
+            near((HD, heads * rows), F32),
+            near((heads * rows, HD), BF16),
+            near((HD, heads * rows), BF16),
+            near((2, heads * rows), F32),
         ),
-        name="prologue",
+        name="prologue", compiler_params=params,
     )(query_raw[0], attn_out[0], out_grad[0], log_totals[0], query_gain)
-    in_vmem = pl.BlockSpec(memory_space=pltpu.VMEM)
     dqt, parts = pl.pallas_call(
         attention,
-        out_shape=(shape((HD, heads * rows), F32), shape((blocks, rows + TAIL, 2 * HD), BF16)),
+        out_shape=(
+            near((HD, heads * rows), F32),
+            near((blocks, rows + TAIL, 2 * HD), BF16),
+        ),
         in_specs=[pl.BlockSpec(memory_space=pltpu.SMEM)] + [in_vmem] * 8,
         scratch_shapes=[
             pltpu.VMEM((blocks // 2, 2 * rows, HD), BF16),
             pltpu.VMEM((blocks // 2, HD, 2 * rows), BF16),
             pltpu.VMEM((blocks // 2, 2 * rows, HD), F32),
         ],
-        name="attention",
-    )(lax.axis_index("ctx").reshape(1).astype(jnp.int32), gathered, *prepared, key_gain)
-    returned = lax.all_to_all(parts, "ctx", 0, 0, tiled=True)
+        name="attention", compiler_params=params,
+    )(lax.axis_index("ctx").reshape(1).astype(jnp.int32), local_memory(gathered), *prepared, key_gain)
+    returned = exchange(parts, "ctx", blocks, CTX_FIRST)
     grad_query = pl.pallas_call(
-        query_end, out_shape=shape((rows, width), F32), name="query_end"
+        query_end, out_shape=shape((rows, width), F32), name="query_end", compiler_params=params
     )(dqt, query_raw[0], query_gain)
     gains = pl.pallas_call(
-        near_sum, out_shape=shape((others, 2, HD), F32), name="near_sum"
-    )(returned)
-    gains = lax.all_to_all(gains, ("head", "dp"), 0, 0, tiled=True)
+        near_sum, out_shape=near((others, 2, HD), BF16), name="near_sum", compiler_params=params
+    )(local_memory(returned))
+    gains = exchange(gains, ("head", "dp"), others, FAR_FIRST)
     grad_key, grad_value = pl.pallas_call(
         key_end,
         out_shape=(shape((rows, HD), F32), shape((rows, HD), F32)),
-        name="key_end",
-    )(returned, key_raw[0], key_gain)
+        name="key_end", compiler_params=params,
+    )(local_memory(returned), key_raw[0], key_gain)
     pair_count = query_raw.shape[0] * rows * blocks * heads * others
     gains = pl.pallas_call(
         functools.partial(far_sum, factor=1.0 / math.sqrt(pair_count)),
         out_shape=shape((2, HD), F32),
-        name="far_sum",
-    )(gains)
+        name="far_sum", compiler_params=params,
+    )(local_memory(gains))
     return (grad_query[None], grad_key[None], grad_value[None], gains)
 
 

time: 120 us -> 98.6 us (0.82)
  waiting for transfers between devices: 29.2 us -> 13 us
  Pallas kernels: 17.6 us -> 7.63 us
  starting transfers between devices: 48 us -> 53.4 us
    all_to_all x2, waiting for transfers between devices: 29.2 us -> 13 us  [exchange(): lax.all_to_all(values, axes, 0, 0, axis_index_groups=order, tiled=True)]
    pallas_call x4, Pallas kernels: 11.1 us -> 4.37 us  [the longest x1 1.99 us: local(): pl.pallas_call(attention, out_shape=(near((HD, heads * rows), F32), near(...]
    all_to_all x2, starting transfers between devices: 48 us -> 53.4 us  [exchange(): lax.all_to_all(values, axes, 0, 0, axis_index_groups=order, tiled=True)]
    pallas_call x1, Pallas kernels: 2.13 us -> 0.87 us  [local(): pl.pallas_call(key_end, out_shape=(shape((rows, HD), F32), shape((rows, H...]
  transfers between devices with their start and end apart: 2 -> 2, of which waited for: 2 -> 2; matrix products, arithmetic and copies ran while one was open for 0% -> 0% of each run, Pallas kernels for 6% -> 3%
where the time goes in v2:
time: 98.6 us; the launch traced here: 98.2 us
  starting transfers between devices  53.4 us (54%)
  blocking collectives  21.9 us (22%)
  waiting for transfers between devices  13 us (13%)
  Pallas kernels  7.63 us (8%)
  local copies, waits for them, and re-layouts  1.54 us (2%)
    all_to_all x2, starting transfers between devices, exchange(): lax.all_to_all(values, axes, 0, 0, axis_index_groups=order, tiled=True)  53.4 us
    all_to_all x1, blocking collectives, exchange(): lax.all_to_all(values, axes, 0, 0, axis_index_groups=order, tiled=True)  21.9 us
    all_to_all x2, waiting for transfers between devices, exchange(): lax.all_to_all(values, axes, 0, 0, axis_index_groups=order, tiled=True)  13 us
    pallas_call x1, Pallas kernels, local(): pl.pallas_call(attention, out_shape=(near((HD, heads * rows), F32), near(...  1.99 us
  transfers between devices with their start and end apart: 2, of which 2 were waited for; matrix products, arithmetic and copies ran while one was open for 0% of the time, Pallas kernels for 3%

profile of v2, /device:TPU:1, one launch (start us, length us, event | category | flops | bytes accessed | tf_op | source)
XLA Modules:
  0.0 98.2 jit_solution(4958339075446717421)
XLA Ops:
  0.6 0.0 copy-start.3
  0.6 0.7 copy-done.3
  1.4 0.0 copy-start.5
  1.4 0.8 copy-done.5
  2.1 1.1 %spread_rows.1 = bf16[16,128,256]{2,1,0:T(8,128)(2,1)} custom-call(bf16[128,128]{1,0:T(8,128)(2,1)S(1)} %bitcast.16, bf16[128,128]{1,0:T(8,128)(2,1)S(1)} %bitcast.18), custom_call_target="tpu_custom_call" | custom-call | tf_op jit(solution)/shard_map/spread_rows/pallas_call | solution.py:186
  3.2 0.0 copy-start
  3.2 0.0 copy-start.1
  3.2 0.0 copy-start.2
  3.2 0.0 copy-start.6
  3.2 0.0 copy-start.8
  3.3 0.0 copy-start.7
  3.3 9.8 %all-to-all-start = ((bf16[16,128,256]{2,1,0:T(8,128)(2,1)}), bf16[16,128,256]{2,1,0:T(8,128)(2,1)S(1)}, u32[]{:S(2)}, u32[]{:S(2)}) async-start(bf16[16,128,256]{2,1,0:T(8,128)(2,1)} %spread_rows.1), calls=%async_computation | async-start | bytes 2097152 | tf_op jit(solution)/shard_map/all_to_all | solution.py:172
  13.1 0.0 copy-done
  13.1 0.0 copy-done.1
  13.1 0.0 copy-done.2
  13.1 0.0 copy-done.6
  13.1 0.0 copy-done.8
  13.1 0.7 prologue.1
  13.8 7.0 %all-to-all-done.kv_ref = bf16[16,128,256]{2,1,0:T(8,128)(2,1)S(1)} async-done(((bf16[16,128,256]{2,1,0:T(8,128)(2,1)}), bf16[16,128,256]{2,1,0:T(8,128)(2,1)S(1)}, u32[]{:S(2)}, u32[]{:S(2)}) %all-to-all-start) | async-done | bytes 1048608 | tf_op jit(solution)/shard_map/all_to_all | solution.py:172
  20.8 0.0 copy-done.7
  20.8 2.0 %attention.1 = (f32[128,1024]{1,0:T(8,128)S(1)}, bf16[16,136,256]{2,1,0:T(8,128)(2,1)S(1)}) custom-call(s32[1]{0:T(128)} %bitcast.block_ref, bf16[16,128,256]{2,1,0:T(8,128)(2,1)S(1)} %all-to-all-done.kv_ref, bf16[1024,128]{1,0:T(8,128)(2,1)S(1)} %get-tuple-element.14.qn_ref, bf16[128,1024]{1,0:T(8,128)(2,1)S(1)} %get-tuple-element.15.qt_ref, ...), custom_call_target="tpu_custom_call" | custom-call | tf_op jit(solution)/shard_map/attention/pallas_call | solution.py:202
  22.8 21.9 %all_to_all.15.parts_ref = bf16[16,136,256]{2,1,0:T(8,128)(2,1)S(1)} all-to-all(bf16[16,136,256]{2,1,0:T(8,128)(2,1)S(1)} %get-tuple-element.21), channel_id=1, replica_groups={{640,704,768,832,896,960,0,64,128,192,256,320,384,448,512,576},{641,705..., dimensions={0} | all-to-all | bytes 2228224 | tf_op jit(solution)/shard_map/all_to_all | solution.py:172
  44.7 0.0 copy-start.4
  44.7 0.6 near_sum.1
  45.4 43.6 %all-to-all-start.2 = ((bf16[64,2,128]{2,1,0:T(2,128)(2,1)}), bf16[64,2,128]{2,1,0:T(2,128)(2,1)S(1)}, u32[]{:S(2)}, u32[]{:S(2)}) async-start(bf16[64,2,128]{2,1,0:T(2,128)(2,1)} %near_sum.1), calls=%async_computation.2 | async-start | bytes 65536 | tf_op jit(solution)/shard_map/all_to_all | solution.py:172
  89.0 1.8 %query_end.1 = f32[128,1024]{1,0:T(8,128)} custom-call(f32[128,1024]{1,0:T(8,128)S(1)} %get-tuple-element.20.dqt_ref, bf16[128,1024]{1,0:T(8,128)(2,1)S(1)} %bitcast.13, f32[1,128]{1,0:T(1,128)S(1)} %bitcast.23), custom_call_target="tpu_custom_call" | custom-call | tf_op jit(solution)/shard_map/query_end/pallas_call | solution.py:217
  90.7 0.0 copy-done.4
  90.7 0.9 key_end.1
  91.6 6.0 %all-to-all-done.2.gains_ref = bf16[64,2,128]{2,1,0:T(2,128)(2,1)S(1)} async-done(((bf16[64,2,128]{2,1,0:T(2,128)(2,1)}), bf16[64,2,128]{2,1,0:T(2,128)(2,1)S(1)}, u32[]{:S(2)}, u32[]{:S(2)}) %all-to-all-start.2) | async-done | bytes 32800 | tf_op jit(solution)/shard_map/all_to_all | solution.py:172
  97.6 0.6 far_sum.1
Async XLA Ops:
  0.6 0.8 copy-start.3
  1.4 0.8 copy-start.5
  3.2 9.8 %copy-start = (bf16[1,128,1024]{2,1,0:T(8,128)(2,1)S(1)}, bf16[1,128,1024]{2,1,0:T(8,128)(2,1)}, u32[]{:S(2)}) copy-start(bf16[1,128,1024]{2,1,0:T(8,128)(2,1)} %param.8) | copy-start | bytes 786436
  3.2 9.9 %copy-start.1 = (bf16[1,128,1024]{2,1,0:T(8,128)(2,1)S(1)}, bf16[1,128,1024]{2,1,0:T(8,128)(2,1)}, u32[]{:S(2)}) copy-start(bf16[1,128,1024]{2,1,0:T(8,128)(2,1)} %param.11) | copy-start | bytes 786436
  3.2 9.9 %copy-start.2 = (bf16[1,128,1024]{2,1,0:T(8,128)(2,1)S(1)}, bf16[1,128,1024]{2,1,0:T(8,128)(2,1)}, u32[]{:S(2)}) copy-start(bf16[1,128,1024]{2,1,0:T(8,128)(2,1)} %param.12) | copy-start | bytes 786436
  3.2 9.9 %copy-start.6 = (f32[1,8,128]{2,1,0:T(8,128)S(1)}, f32[1,8,128]{2,1,0:T(8,128)}, u32[]{:S(2)}) copy-start(f32[1,8,128]{2,1,0:T(8,128)} %param.13) | copy-start | bytes 12292
  3.2 9.9 %copy-start.8 = (f32[128]{0:T(128)S(1)}, f32[128]{0:T(128)}, u32[]{:S(2)}) copy-start(f32[128]{0:T(128)} %param.14) | copy-start | bytes 1540
  3.3 17.6 %copy-start.7 = (f32[128]{0:T(128)S(1)}, f32[128]{0:T(128)}, u32[]{:S(2)}) copy-start(f32[128]{0:T(128)} %param.15) | copy-start | bytes 1540
  3.3 17.6 %all-to-all-start = ((bf16[16,128,256]{2,1,0:T(8,128)(2,1)}), bf16[16,128,256]{2,1,0:T(8,128)(2,1)S(1)}, u32[]{:S(2)}, u32[]{:S(2)}) async-start(bf16[16,128,256]{2,1,0:T(8,128)(2,1)} %spread_rows.1), calls=%async_computation | async-start | bytes 2097152 | tf_op jit(solution)/shard_map/all_to_all | solution.py:172
  44.7 46.0 %copy-start.4 = (bf16[1,128,128]{2,1,0:T(8,128)(2,1)S(1)}, bf16[1,128,128]{2,1,0:T(8,128)(2,1)}, u32[]{:S(2)}) copy-start(bf16[1,128,128]{2,1,0:T(8,128)(2,1)} %param.9) | copy-start | bytes 98308
  45.4 52.2 %all-to-all-start.2 = ((bf16[64,2,128]{2,1,0:T(2,128)(2,1)}), bf16[64,2,128]{2,1,0:T(2,128)(2,1)S(1)}, u32[]{:S(2)}, u32[]{:S(2)}) async-start(bf16[64,2,128]{2,1,0:T(2,128)(2,1)} %near_sum.1), calls=%async_computation.2 | async-start | bytes 65536 | tf_op jit(solution)/shard_map/all_to_all | solution.py:172

commit v3 on v2

v3 whole, which is shorter than its diff:
```python
import functools
import math

import jax
import jax.numpy as jnp
from jax import lax
from jax.experimental import pallas as pl
from jax.experimental.pallas import tpu as pltpu
from jax.sharding import PartitionSpec as P

HD = 128
TAIL = 8
VMEM_LIMIT = 32 * 2**20
GATHER_FIRST = 10
GATHER_TURN = 3
BACK_FIRST = 14
BACK_TURN = 1
KEY_BLOCKS = 4
AHEAD = 1
Q_ROWS = 512
FAR_FIRST = 40
EPS = 1e-06
LOG2E = 1.4426950408889634
F32 = jnp.float32
BF16 = jnp.bfloat16


def prologue(q_ref, o_ref, g_ref, lt_ref, qgain_ref, qn_ref, qt_ref, un_ref, gt_ref, lse_ref, delta_ref):
    rows = q_ref.shape[0]
    for h in range(q_ref.shape[1] // HD):
        cols = slice(h * HD, (h + 1) * HD)
        span = slice(h * rows, (h + 1) * rows)
        q = q_ref[:, cols].astype(F32)
        inverse = lax.rsqrt(jnp.mean(q * q, axis=-1, keepdims=True) + EPS)
        unit = q * inverse
        un_ref[span, :] = unit
        qn = (unit * qgain_ref[...]).astype(BF16)
        qn_ref[span, :] = qn
        qt_ref[:, span] = qn.astype(F32).T.astype(BF16)
        g = g_ref[:, cols].astype(F32)
        gt_ref[:, span] = g.T.astype(BF16)
        delta = jnp.sum(g * o_ref[:, cols].astype(F32), axis=-1, keepdims=True)
        delta_ref[span, :] = jnp.broadcast_to(delta, (rows, HD))
        lse_ref[span, :] = jnp.broadcast_to(lt_ref[h : h + 1, :] * LOG2E, (HD, rows)).T


def attention(
    block_ref, kv_ref, qn_ref, qt_ref, un_ref, gt_ref, lse_ref, delta_ref, g_ref, kgain_ref,
    dq_ref, parts_ref,
    kn_ref, kt_ref, vt_ref, unit_ref,
):
    blocks, rows = kv_ref.shape[0], kv_ref.shape[1]
    width = qt_ref.shape[1]
    scale = 1.0 / math.sqrt(HD)
    pair = KEY_BLOCKS * rows
    twos = KEY_BLOCKS // 2
    wide = Q_ROWS
    block = block_ref[0]
    last = block // KEY_BLOCKS

    def prepare(j):
        ats = [(j * twos + i + GATHER_TURN) % (blocks // 2) for i in range(twos)]
        kv = [kv_ref[pl.ds(2 * at, 2)].reshape(2 * rows, 2 * HD) for at in ats]
        kv = jnp.concatenate(kv, axis=0).astype(F32)
        k = kv[:, :HD]
        v = kv[:, HD:]
        inverse = lax.rsqrt(jnp.mean(k * k, axis=-1, keepdims=True) + EPS)
        unit = k * inverse
        kn = (unit * kgain_ref[...]).astype(BF16)
        slot = j % 2
        unit_ref[slot] = unit
        kn_ref[slot] = kn
        kt_ref[slot] = kn.astype(F32).T.astype(BF16)
        vt_ref[slot] = v.T.astype(BF16)

    def step(j, k_gain, masked):
        slot = j % 2
        kn = kn_ref[slot]
        kt = kt_ref[slot]
        vt = vt_ref[slot]
        unit = unit_ref[slot]
        dkt = jnp.zeros((HD, pair), F32)
        dvt = jnp.zeros((HD, pair), F32)
        if masked:
            key_pos = j * pair + lax.broadcasted_iota(jnp.int32, (wide, pair), 1)
            query_pos = block * rows + lax.broadcasted_iota(jnp.int32, (wide, pair), 0) % rows
            keep = key_pos <= query_pos
        chunks = width // wide
        spans = [slice(c * wide, (c + 1) * wide) for c in range(chunks)]
        across = pair // HD

        def products(c):
            heads = range(c * wide // rows, (c + 1) * wide // rows)
            g = jnp.concatenate([g_ref[:, h * HD : (h + 1) * HD] for h in heads], axis=0)
            scores = jnp.dot(qn_ref[spans[c], :], kt, preferred_element_type=F32)
            return scores, jnp.dot(g, vt, preferred_element_type=F32)

        def weights(c, scores, dp):
            lse = jnp.concatenate([lse_ref[spans[c], :]] * across, axis=1)
            delta = jnp.concatenate([delta_ref[spans[c], :]] * across, axis=1)
            probs = jnp.exp2(scores * (scale * LOG2E) - lse)
            if masked:
                probs = jnp.where(keep, probs, 0.0)
            return probs.astype(BF16), (probs * (dp - delta)).astype(BF16)

        ahead = [products(c) for c in range(AHEAD)]
        for c in range(chunks):
            if c + AHEAD < chunks:
                ahead.append(products(c + AHEAD))
            low, ds = weights(c, *ahead[c])
            dvt += jnp.dot(gt_ref[:, spans[c]], low, preferred_element_type=F32)
            dkt += jnp.dot(qt_ref[:, spans[c]], ds, preferred_element_type=F32)
            dq_ref[spans[c], :] += jnp.dot(ds, kn, preferred_element_type=F32)
        dk = dkt.T * scale
        dv = dvt.T
        for i in range(twos):
            at = (j * twos + i + BACK_TURN) % (blocks // 2)
            piece = slice(2 * i * rows, 2 * (i + 1) * rows)
            parts_ref[pl.ds(2 * at, 2), :rows, :HD] = dk[piece].astype(BF16).reshape(2, rows, HD)
            parts_ref[pl.ds(2 * at, 2), :rows, HD:] = dv[piece].astype(BF16).reshape(2, rows, HD)
        if not masked:
            prepare(j + 1)
        return k_gain + jnp.sum(dk * unit, axis=0, keepdims=True)

    prepare(0)
    dq_ref[...] = jnp.zeros(dq_ref.shape, F32)
    k_gain = lax.fori_loop(0, last, lambda j, s: step(j, s, False), jnp.zeros((1, HD), F32))
    k_gain = step(last, k_gain, True)

    def clear(j, carry):
        at = (j + BACK_TURN) % (blocks // 2)
        parts_ref[pl.ds(2 * at, 2), :rows] = jnp.zeros((2, rows, 2 * HD), BF16)
        return carry

    lax.fori_loop((last + 1) * twos, blocks // 2, clear, 0)
    product = jnp.zeros((rows, HD), F32)
    for h in range(width // rows):
        span = slice(h * rows, (h + 1) * rows)
        product += dq_ref[span, :] * un_ref[span, :]
    q_gain = jnp.sum(product, axis=0, keepdims=True) * scale
    sums = jnp.concatenate([q_gain, k_gain], axis=1)
    high = sums.astype(BF16).astype(F32)
    middle = (sums - high).astype(BF16).astype(F32)
    low = sums - high - middle
    tail = jnp.concatenate([high, middle, low, jnp.zeros((TAIL - 3, 2 * HD), F32)], axis=0)
    tail = tail.astype(BF16)
    for b in range(blocks):
        parts_ref[b, rows:] = tail


def query_end(dq_ref, q_ref, qgain_ref, gq_ref):
    rows = q_ref.shape[0]
    scale = 1.0 / math.sqrt(HD)
    for h in range(q_ref.shape[1] // HD):
        cols = slice(h * HD, (h + 1) * HD)
        grad_norm = dq_ref[h * rows : (h + 1) * rows, :] * scale
        q = q_ref[:, cols].astype(F32)
        inverse = lax.rsqrt(jnp.mean(q * q, axis=-1, keepdims=True) + EPS)
        unit = q * inverse
        grad_unit = grad_norm * qgain_ref[...]
        mean = jnp.mean(grad_unit * unit, axis=-1, keepdims=True)
        gq_ref[:, cols] = (grad_unit - unit * mean) * inverse


def near_sum(parts_ref, gains_ref):
    total = parts_ref[0, -TAIL:].astype(F32)
    for b in range(1, parts_ref.shape[0]):
        total += parts_ref[b, -TAIL:].astype(F32)
    sums = jnp.sum(total, axis=0, keepdims=True)
    sums = jnp.concatenate([sums[:, :HD], sums[:, HD:]], axis=0).astype(BF16)
    for i in range(gains_ref.shape[0]):
        gains_ref[i] = sums


def far_sum(gains_ref, out_ref, *, factor):
    out_ref[...] = jnp.sum(gains_ref[...].astype(F32), axis=0) * factor


def key_end(parts_ref, k_ref, kgain_ref, gk_ref, gv_ref):
    rows = k_ref.shape[0]
    total = parts_ref[0, :rows].astype(F32)
    for b in range(1, parts_ref.shape[0]):
        total += parts_ref[b, :rows].astype(F32)
    grad_norm = total[:, :HD]
    gv_ref[...] = total[:, HD:]
    k = k_ref[...].astype(F32)
    inverse = lax.rsqrt(jnp.mean(k * k, axis=-1, keepdims=True) + EPS)
    unit = k * inverse
    grad_unit = grad_norm * kgain_ref[...]
    mean = jnp.mean(grad_unit * unit, axis=-1, keepdims=True)
    gk_ref[...] = (grad_unit - unit * mean) * inverse


def spread_rows(k_ref, v_ref, out_ref, both_ref, in_sem, out_sem):
    halves = (slice(0, HD), slice(HD, 2 * HD))
    ins = [
        pltpu.make_async_copy(ref, both_ref.at[:, half], in_sem.at[i])
        for i, (ref, half) in enumerate(zip((k_ref, v_ref), halves))
    ]
    for copy in ins:
        copy.start()
    for copy in ins:
        copy.wait()
    outs = [
        pltpu.make_async_copy(both_ref, out_ref.at[b], out_sem.at[b])
        for b in range(out_ref.shape[0])
    ]
    for copy in outs:
        copy.start()
    for copy in outs:
        copy.wait()


def local_memory(values):
    return pltpu.with_memory_space_constraint(values, pltpu.VMEM)


def far_memory(values):
    return pltpu.with_memory_space_constraint(values, pltpu.HBM)


def exchange(values, axes, count, first):
    order = [[(first + i) % count for i in range(count)]]
    return lax.all_to_all(values, axes, 0, 0, axis_index_groups=order, tiled=True)


def local(query_raw, key_raw, value_rows, attn_out, out_grad, log_totals, query_gain, key_gain):
    blocks = lax.axis_size("ctx")
    rows, width = query_raw.shape[1], query_raw.shape[2]
    heads = width // HD
    others = lax.axis_size("head") * lax.axis_size("dp")
    shape = jax.ShapeDtypeStruct
    near = pltpu.VMEM
    params = pltpu.CompilerParams(vmem_limit_bytes=VMEM_LIMIT)
    in_vmem = pl.BlockSpec(memory_space=pltpu.VMEM)
    query_gain = query_gain.reshape(1, HD)
    key_gain = key_gain.reshape(1, HD)
    in_hbm = pl.BlockSpec(memory_space=pltpu.HBM)
    spread = pl.pallas_call(
        spread_rows,
        in_specs=[in_hbm, in_hbm],
        out_specs=in_hbm,
        out_shape=shape((blocks, rows, 2 * HD), BF16),
        scratch_shapes=[
            pltpu.VMEM((rows, 2 * HD), BF16),
            pltpu.SemaphoreType.DMA((2,)),
            pltpu.SemaphoreType.DMA((blocks,)),
        ],
        name="spread_rows",
        compiler_params=params,
    )(far_memory(key_raw[0]), far_memory(value_rows[0]))
    gathered = exchange(spread, "ctx", blocks, GATHER_FIRST)
    prepared = pl.pallas_call(
        prologue,
        out_shape=(
            near((heads * rows, HD), BF16),
            near((HD, heads * rows), BF16),
            near((heads * rows, HD), F32),
            near((HD, heads * rows), BF16),
            near((heads * rows, HD), F32),
            near((heads * rows, HD), F32),
        ),
        name="prologue", compiler_params=params,
    )(query_raw[0], attn_out[0], out_grad[0], log_totals[0], query_gain)
    dq, parts = pl.pallas_call(
        attention,
        out_shape=(near((heads * rows, HD), F32), near((blocks, rows + TAIL, 2 * HD), BF16)),
        in_specs=[pl.BlockSpec(memory_space=pltpu.SMEM)] + [in_vmem] * 9,
        scratch_shapes=[
            pltpu.VMEM((2, KEY_BLOCKS * rows, HD), BF16),
            pltpu.VMEM((2, HD, KEY_BLOCKS * rows), BF16),
            pltpu.VMEM((2, HD, KEY_BLOCKS * rows), BF16),
            pltpu.VMEM((2, KEY_BLOCKS * rows, HD), F32),
        ],
        name="attention", compiler_params=params,
    )(lax.axis_index("ctx").reshape(1).astype(jnp.int32), local_memory(gathered), *prepared, out_grad[0], key_gain)
    returned = exchange(parts, "ctx", blocks, BACK_FIRST)
    grad_query = pl.pallas_call(
        query_end, out_shape=shape((rows, width), F32), name="query_end", compiler_params=params
    )(dq, query_raw[0], query_gain)
    gains = pl.pallas_call(
        near_sum, out_shape=near((others, 2, HD), BF16), name="near_sum", compiler_params=params
    )(local_memory(returned))
    gains = exchange(gains, ("head", "dp"), others, FAR_FIRST)
    grad_key, grad_value = pl.pallas_call(
        key_end,
        out_shape=(shape((rows, HD), F32), shape((rows, HD), F32)),
        name="key_end", compiler_params=params,
    )(local_memory(returned), key_raw[0], key_gain)
    pair_count = query_raw.shape[0] * rows * blocks * heads * others
    gains = pl.pallas_call(
        functools.partial(far_sum, factor=1.0 / math.sqrt(pair_count)),
        out_shape=shape((2, HD), F32),
        name="far_sum", compiler_params=params,
    )(local_memory(gains))
    return (grad_query[None], grad_key[None], grad_value[None], gains)


def solution(mesh):
    return jax.shard_map(
        local,
        mesh=mesh,
        in_specs=(
            P("dp", "ctx", "head"),
            P("dp", "ctx", "head"),
            P("dp", "ctx", "head"),
            P("dp", "ctx", "head"),
            P("dp", "ctx", "head"),
            P("dp", "head", "ctx"),
            P(),
            P(),
        ),
        out_specs=(P("dp", "ctx", "head"), P("dp", "ctx", "head"), P("dp", "ctx", "head"), P()),
        check_vma=False,
    )
```

time: 98.6 us -> 96.8 us (0.982)
  blocking collectives: 21.9 us -> 17.7 us
  local copies, waits for them, and re-layouts: 1.54 us -> 5.2 us
  waiting for transfers between devices: 13 us -> 11.1 us
    all_to_all x1, blocking collectives: 21.9 us -> 17.7 us  [exchange(): lax.all_to_all(values, axes, 0, 0, axis_index_groups=order, tiled=True)]
    unnamed x18 -> x26, local copies, waits for them, and re-layouts: 1.54 us -> 5.2 us
    all_to_all x2, waiting for transfers between devices: 13 us -> 11.1 us  [exchange(): lax.all_to_all(values, axes, 0, 0, axis_index_groups=order, tiled=True)]
where the time goes in v3:
time: 96.8 us; the launch traced here: 96.3 us
  starting transfers between devices  53.4 us (55%)
  blocking collectives  17.7 us (18%)
  waiting for transfers between devices  11.1 us (11%)
  Pallas kernels  8.12 us (8%)
  local copies, waits for them, and re-layouts  5.2 us (5%)
    all_to_all x2, starting transfers between devices, exchange(): lax.all_to_all(values, axes, 0, 0, axis_index_groups=order, tiled=True)  53.4 us
    all_to_all x1, blocking collectives, exchange(): lax.all_to_all(values, axes, 0, 0, axis_index_groups=order, tiled=True)  17.7 us
    all_to_all x2, waiting for transfers between devices, exchange(): lax.all_to_all(values, axes, 0, 0, axis_index_groups=order, tiled=True)  11.1 us
    unnamed x26, local copies, waits for them, and re-layouts  5.2 us
    pallas_call x1, Pallas kernels, local(): pl.pallas_call(attention, out_shape=(near((heads * rows, HD), F32), near(...  2 us
  transfers between devices with their start and end apart: 2, of which 2 were waited for; matrix products, arithmetic and copies ran while one was open for 0% of the time, Pallas kernels for 3%

profile of v3, /device:TPU:1, one launch (start us, length us, event | category | flops | bytes accessed | tf_op | source)
XLA Modules:
  0.0 96.3 jit_solution(15067688764977918661)
XLA Ops:
  0.6 1.9 %spread_rows.1 = bf16[16,128,256]{2,1,0:T(8,128)(2,1)} custom-call(bf16[128,128]{1,0:T(8,128)(2,1)} %bitcast.17, bf16[128,128]{1,0:T(8,128)(2,1)} %bitcast.25), custom_call_target="tpu_custom_call" | custom-call | tf_op jit(solution)/shard_map/spread_rows/pallas_call | solution.py:239
  2.6 0.0 copy-start
  2.6 0.0 copy-start.1
  2.6 0.0 copy-start.4
  2.6 0.0 copy-start.10
  2.6 0.0 copy-start.12
  2.6 0.0 copy-start.11
  2.6 9.8 %all-to-all-start = ((bf16[16,128,256]{2,1,0:T(8,128)(2,1)}), bf16[16,128,256]{2,1,0:T(8,128)(2,1)S(1)}, u32[]{:S(2)}, u32[]{:S(2)}) async-start(bf16[16,128,256]{2,1,0:T(8,128)(2,1)} %spread_rows.1), calls=%async_computation | async-start | bytes 2097152 | tf_op jit(solution)/shard_map/all_to_all | solution.py:224
  12.4 0.0 copy-done
  12.4 0.0 copy-done.1
  12.4 0.0 copy-done.4
  12.5 0.0 copy-done.10
  12.5 0.0 copy-done.12
  12.5 0.7 prologue.1
  13.2 0.0 copy-start.2
  13.2 0.8 copy-done.2
  14.0 0.0 copy-start.5
  14.0 0.7 copy-done.5
  14.7 0.0 copy-start.7
  14.7 0.7 copy-done.7
  15.4 4.8 %all-to-all-done.kv_ref = bf16[16,128,256]{2,1,0:T(8,128)(2,1)S(1)} async-done(((bf16[16,128,256]{2,1,0:T(8,128)(2,1)}), bf16[16,128,256]{2,1,0:T(8,128)(2,1)S(1)}, u32[]{:S(2)}, u32[]{:S(2)}) %all-to-all-start) | async-done | bytes 1048608 | tf_op jit(solution)/shard_map/all_to_all | solution.py:224
  20.2 0.0 copy-done.11
  20.2 0.0 copy-start.3
  20.2 1.0 %copy-done.3 = f32[1024,128]{1,0:T(8,128)S(1)} copy-done((f32[1024,128]{1,0:T(8,128)S(1)}, f32[1024,128]{1,0:T(8,128)}, u32[]{:S(2)}) %copy-start.3) | copy-done | bytes 524312
  21.2 0.0 copy-start.6
  21.2 0.9 copy-done.6
  22.2 0.0 copy-start.8
  22.2 0.9 copy-done.8
  23.1 2.0 %attention.1 = (f32[1024,128]{1,0:T(8,128)S(1)}, bf16[16,136,256]{2,1,0:T(8,128)(2,1)S(1)}) custom-call(s32[1]{0:T(128)} %bitcast.block_ref, bf16[16,128,256]{2,1,0:T(8,128)(2,1)S(1)} %all-to-all-done.kv_ref, bf16[1024,128]{1,0:T(8,128)(2,1)S(1)} %get-tuple-element.14.qn_ref, bf16[128,1024]{1,0:T(8,128)(2,1)S(1)} %copy-done.6, ...), custom_call_target="tpu_custom_call" | custom-call | tf_op jit(solution)/shard_map/attention/pallas_call | solution.py:265
  25.1 17.7 %all_to_all.15.parts_ref = bf16[16,136,256]{2,1,0:T(8,128)(2,1)S(1)} all-to-all(bf16[16,136,256]{2,1,0:T(8,128)(2,1)S(1)} %get-tuple-element.21), channel_id=1, replica_groups={{896,960,0,64,128,192,256,320,384,448,512,576,640,704,768,832},{897,961..., dimensions={0} | all-to-all | bytes 2228224 | tf_op jit(solution)/shard_map/all_to_all | solution.py:224
  42.8 0.0 copy-start.9
  42.8 0.7 near_sum.1
  43.5 43.6 %all-to-all-start.2 = ((bf16[64,2,128]{2,1,0:T(2,128)(2,1)}), bf16[64,2,128]{2,1,0:T(2,128)(2,1)S(1)}, u32[]{:S(2)}, u32[]{:S(2)}) async-start(bf16[64,2,128]{2,1,0:T(2,128)(2,1)} %near_sum.1), calls=%async_computation.2 | async-start | bytes 65536 | tf_op jit(solution)/shard_map/all_to_all | solution.py:224
  87.1 1.4 %query_end.1 = f32[128,1024]{1,0:T(8,128)} custom-call(f32[1024,128]{1,0:T(8,128)S(1)} %get-tuple-element.20.dq_ref, bf16[128,1024]{1,0:T(8,128)(2,1)S(1)} %bitcast.13, f32[1,128]{1,0:T(1,128)S(1)} %bitcast.23), custom_call_target="tpu_custom_call" | custom-call | tf_op jit(solution)/shard_map/query_end/pallas_call | solution.py:278
  88.4 0.0 copy-done.9
  88.4 0.9 key_end.1
  89.3 6.4 %all-to-all-done.2.gains_ref = bf16[64,2,128]{2,1,0:T(2,128)(2,1)S(1)} async-done(((bf16[64,2,128]{2,1,0:T(2,128)(2,1)}), bf16[64,2,128]{2,1,0:T(2,128)(2,1)S(1)}, u32[]{:S(2)}, u32[]{:S(2)}) %all-to-all-start.2) | async-done | bytes 32800 | tf_op jit(solution)/shard_map/all_to_all | solution.py:224
  95.7 0.6 far_sum.1
Async XLA Ops:
  2.6 9.9 %copy-start = (bf16[1,128,1024]{2,1,0:T(8,128)(2,1)S(1)}, bf16[1,128,1024]{2,1,0:T(8,128)(2,1)}, u32[]{:S(2)}) copy-start(bf16[1,128,1024]{2,1,0:T(8,128)(2,1)} %param.8) | copy-start | bytes 786436
  2.6 9.9 %copy-start.1 = (bf16[1,128,1024]{2,1,0:T(8,128)(2,1)S(1)}, bf16[1,128,1024]{2,1,0:T(8,128)(2,1)}, u32[]{:S(2)}) copy-start(bf16[1,128,1024]{2,1,0:T(8,128)(2,1)} %param.12) | copy-start | bytes 786436
  2.6 9.9 %copy-start.4 = (bf16[1,128,1024]{2,1,0:T(8,128)(2,1)S(1)}, bf16[1,128,1024]{2,1,0:T(8,128)(2,1)}, u32[]{:S(2)}) copy-start(bf16[1,128,1024]{2,1,0:T(8,128)(2,1)} %param.11) | copy-start | bytes 786436
  2.6 9.9 %copy-start.10 = (f32[1,8,128]{2,1,0:T(8,128)S(1)}, f32[1,8,128]{2,1,0:T(8,128)}, u32[]{:S(2)}) copy-start(f32[1,8,128]{2,1,0:T(8,128)} %param.13) | copy-start | bytes 12292
  2.6 9.9 %copy-start.12 = (f32[128]{0:T(128)S(1)}, f32[128]{0:T(128)}, u32[]{:S(2)}) copy-start(f32[128]{0:T(128)} %param.14) | copy-start | bytes 1540
  2.6 17.6 %copy-start.11 = (f32[128]{0:T(128)S(1)}, f32[128]{0:T(128)}, u32[]{:S(2)}) copy-start(f32[128]{0:T(128)} %param.15) | copy-start | bytes 1540
  2.6 17.6 %all-to-all-start = ((bf16[16,128,256]{2,1,0:T(8,128)(2,1)}), bf16[16,128,256]{2,1,0:T(8,128)(2,1)S(1)}, u32[]{:S(2)}, u32[]{:S(2)}) async-start(bf16[16,128,256]{2,1,0:T(8,128)(2,1)} %spread_rows.1), calls=%async_computation | async-start | bytes 2097152 | tf_op jit(solution)/shard_map/all_to_all | solution.py:224
  13.2 0.8 copy-start.2
  14.0 0.7 copy-start.5
  14.7 0.7 copy-start.7
  20.2 1.0 %copy-start.3 = (f32[1024,128]{1,0:T(8,128)S(1)}, f32[1024,128]{1,0:T(8,128)}, u32[]{:S(2)}) copy-start(f32[1024,128]{1,0:T(8,128)} %copy-done.2) | copy-start | bytes 1572868
  21.2 0.9 copy-start.6
  22.2 0.9 copy-start.8
  42.8 45.6 %copy-start.9 = (bf16[1,128,128]{2,1,0:T(8,128)(2,1)S(1)}, bf16[1,128,128]{2,1,0:T(8,128)(2,1)}, u32[]{:S(2)}) copy-start(bf16[1,128,128]{2,1,0:T(8,128)(2,1)} %param.9) | copy-start | bytes 98308
  43.5 52.2 %all-to-all-start.2 = ((bf16[64,2,128]{2,1,0:T(2,128)(2,1)}), bf16[64,2,128]{2,1,0:T(2,128)(2,1)S(1)}, u32[]{:S(2)}, u32[]{:S(2)}) async-start(bf16[64,2,128]{2,1,0:T(2,128)(2,1)} %near_sum.1), calls=%async_computation.2 | async-start | bytes 65536 | tf_op jit(solution)/shard_map/all_to_all | solution.py:224

commit v4 on v3

--- a/solution.py
+++ b/solution.py
@@ -25,31 +25,28 @@
 BF16 = jnp.bfloat16
 
 
-def prologue(q_ref, o_ref, g_ref, lt_ref, qgain_ref, qn_ref, qt_ref, un_ref, gt_ref, lse_ref, delta_ref):
+def prologue(q_ref, o_ref, g_ref, qgain_ref, qn_ref, qt_ref, gt_ref, delta_ref):
     rows = q_ref.shape[0]
     for h in range(q_ref.shape[1] // HD):
         cols = slice(h * HD, (h + 1) * HD)
         span = slice(h * rows, (h + 1) * rows)
         q = q_ref[:, cols].astype(F32)
         inverse = lax.rsqrt(jnp.mean(q * q, axis=-1, keepdims=True) + EPS)
-        unit = q * inverse
-        un_ref[span, :] = unit
-        qn = (unit * qgain_ref[...]).astype(BF16)
+        qn = (q * inverse * qgain_ref[...]).astype(BF16)
         qn_ref[span, :] = qn
         qt_ref[:, span] = qn.astype(F32).T.astype(BF16)
         g = g_ref[:, cols].astype(F32)
         gt_ref[:, span] = g.T.astype(BF16)
         delta = jnp.sum(g * o_ref[:, cols].astype(F32), axis=-1, keepdims=True)
         delta_ref[span, :] = jnp.broadcast_to(delta, (rows, HD))
-        lse_ref[span, :] = jnp.broadcast_to(lt_ref[h : h + 1, :] * LOG2E, (HD, rows)).T
 
 
 def attention(
-    block_ref, kv_ref, qn_ref, qt_ref, un_ref, gt_ref, lse_ref, delta_ref, g_ref, kgain_ref,
+    block_ref, kv_ref, qn_ref, qt_ref, gt_ref, delta_ref, lt_ref, g_ref, q_ref, kgain_ref,
     dq_ref, parts_ref,
-    kn_ref, kt_ref, vt_ref, unit_ref,
+    kn_ref, kt_ref, vt_ref, unit_ref, lse_ref,
 ):
-    blocks, rows = kv_ref.shape[0], kv_ref.shape[1]
+    blocks, rows = kv_ref.shape[0], kv_ref.shape[1] // 2
     width = qt_ref.shape[1]
     scale = 1.0 / math.sqrt(HD)
     pair = KEY_BLOCKS * rows
@@ -60,10 +57,10 @@
 
     def prepare(j):
         ats = [(j * twos + i + GATHER_TURN) % (blocks // 2) for i in range(twos)]
-        kv = [kv_ref[pl.ds(2 * at, 2)].reshape(2 * rows, 2 * HD) for at in ats]
-        kv = jnp.concatenate(kv, axis=0).astype(F32)
-        k = kv[:, :HD]
-        v = kv[:, HD:]
+        k = [kv_ref[pl.ds(2 * at, 2), :rows].reshape(2 * rows, HD) for at in ats]
+        v = [kv_ref[pl.ds(2 * at, 2), rows:].reshape(2 * rows, HD) for at in ats]
+        k = jnp.concatenate(k, axis=0).astype(F32)
+        v = jnp.concatenate(v, axis=0).astype(F32)
         inverse = lax.rsqrt(jnp.mean(k * k, axis=-1, keepdims=True) + EPS)
         unit = k * inverse
         kn = (unit * kgain_ref[...]).astype(BF16)
@@ -123,6 +120,9 @@
         return k_gain + jnp.sum(dk * unit, axis=0, keepdims=True)
 
     prepare(0)
+    for h in range(width // rows):
+        span = slice(h * rows, (h + 1) * rows)
+        lse_ref[span, :] = jnp.broadcast_to(lt_ref[h : h + 1, :] * LOG2E, (HD, rows)).T
     dq_ref[...] = jnp.zeros(dq_ref.shape, F32)
     k_gain = lax.fori_loop(0, last, lambda j, s: step(j, s, False), jnp.zeros((1, HD), F32))
     k_gain = step(last, k_gain, True)
@@ -136,7 +136,9 @@
     product = jnp.zeros((rows, HD), F32)
     for h in range(width // rows):
         span = slice(h * rows, (h + 1) * rows)
-        product += dq_ref[span, :] * un_ref[span, :]
+        q = q_ref[:, h * HD : (h + 1) * HD].astype(F32)
+        inverse = lax.rsqrt(jnp.mean(q * q, axis=-1, keepdims=True) + EPS)
+        product += dq_ref[span, :] * (q * inverse)
     q_gain = jnp.sum(product, axis=0, keepdims=True) * scale
     sums = jnp.concatenate([q_gain, k_gain], axis=1)
     high = sums.astype(BF16).astype(F32)
@@ -191,32 +193,8 @@
     gk_ref[...] = (grad_unit - unit * mean) * inverse
 
 
-def spread_rows(k_ref, v_ref, out_ref, both_ref, in_sem, out_sem):
-    halves = (slice(0, HD), slice(HD, 2 * HD))
-    ins = [
-        pltpu.make_async_copy(ref, both_ref.at[:, half], in_sem.at[i])
-        for i, (ref, half) in enumerate(zip((k_ref, v_ref), halves))
-    ]
-    for copy in ins:
-        copy.start()
-    for copy in ins:
-        copy.wait()
-    outs = [
-        pltpu.make_async_copy(both_ref, out_ref.at[b], out_sem.at[b])
-        for b in range(out_ref.shape[0])
-    ]
-    for copy in outs:
-        copy.start()
-    for copy in outs:
-        copy.wait()
-
-
 def local_memory(values):
     return pltpu.with_memory_space_constraint(values, pltpu.VMEM)
-
-
-def far_memory(values):
-    return pltpu.with_memory_space_constraint(values, pltpu.HBM)
 
 
 def exchange(values, axes, count, first):
@@ -235,33 +213,19 @@
     in_vmem = pl.BlockSpec(memory_space=pltpu.VMEM)
     query_gain = query_gain.reshape(1, HD)
     key_gain = key_gain.reshape(1, HD)
-    in_hbm = pl.BlockSpec(memory_space=pltpu.HBM)
-    spread = pl.pallas_call(
-        spread_rows,
-        in_specs=[in_hbm, in_hbm],
-        out_specs=in_hbm,
-        out_shape=shape((blocks, rows, 2 * HD), BF16),
-        scratch_shapes=[
-            pltpu.VMEM((rows, 2 * HD), BF16),
-            pltpu.SemaphoreType.DMA((2,)),
-            pltpu.SemaphoreType.DMA((blocks,)),
-        ],
-        name="spread_rows",
-        compiler_params=params,
-    )(far_memory(key_raw[0]), far_memory(value_rows[0]))
+    own = jnp.concatenate([key_raw[0], value_rows[0]], axis=0)
+    spread = jnp.broadcast_to(own[None], (blocks, 2 * rows, HD))
     gathered = exchange(spread, "ctx", blocks, GATHER_FIRST)
     prepared = pl.pallas_call(
         prologue,
         out_shape=(
             near((heads * rows, HD), BF16),
             near((HD, heads * rows), BF16),
-            near((heads * rows, HD), F32),
             near((HD, heads * rows), BF16),
-            near((heads * rows, HD), F32),
             near((heads * rows, HD), F32),
         ),
         name="prologue", compiler_params=params,
-    )(query_raw[0], attn_out[0], out_grad[0], log_totals[0], query_gain)
+    )(query_raw[0], attn_out[0], out_grad[0], query_gain)
     dq, parts = pl.pallas_call(
         attention,
         out_shape=(near((heads * rows, HD), F32), near((blocks, rows + TAIL, 2 * HD), BF16)),
@@ -271,9 +235,10 @@
             pltpu.VMEM((2, HD, KEY_BLOCKS * rows), BF16),
             pltpu.VMEM((2, HD, KEY_BLOCKS * rows), BF16),
             pltpu.VMEM((2, KEY_BLOCKS * rows, HD), F32),
+            pltpu.VMEM((heads * rows, HD), F32),
         ],
         name="attention", compiler_params=params,
-    )(lax.axis_index("ctx").reshape(1).astype(jnp.int32), local_memory(gathered), *prepared, out_grad[0], key_gain)
+    )(lax.axis_index("ctx").reshape(1).astype(jnp.int32), local_memory(gathered), *prepared, log_totals[0], out_grad[0], query_raw[0], key_gain)
     returned = exchange(parts, "ctx", blocks, BACK_FIRST)
     grad_query = pl.pallas_call(
         query_end, out_shape=shape((rows, width), F32), name="query_end", compiler_params=params

time: 96.8 us -> 94.2 us (0.973)
  local copies, waits for them, and re-layouts: 5.2 us -> 1.21 us
  waiting for transfers between devices: 11.1 us -> 13.5 us
  Pallas kernels: 8.12 us -> 6.4 us
    unnamed x26 -> x14, local copies, waits for them, and re-layouts: 5.2 us -> 0.03 us
    all_to_all x2, waiting for transfers between devices: 11.1 us -> 13.5 us  [exchange(): lax.all_to_all(values, axes, 0, 0, axis_index_groups=order, tiled=True)]
    pallas_call x1 -> x0, Pallas kernels: 1.91 us -> none  [local(): pl.pallas_call(spread_rows, in_specs=[in_hbm, in_hbm], out_specs=in_hbm,...]
    broadcast_in_dim x0 -> x1, local copies, waits for them, and re-layouts: none -> 1.17 us  [local(): spread = jnp.broadcast_to(own[None], (blocks, 2 * rows, HD))]
where the time goes in v4:
time: 94.2 us; the launch traced here: 93.8 us
  starting transfers between devices  53.5 us (57%)
  blocking collectives  17.7 us (19%)
  waiting for transfers between devices  13.5 us (14%)
  Pallas kernels  6.4 us (7%)
  local copies, waits for them, and re-layouts  1.21 us (1%)
    all_to_all x2, starting transfers between devices, exchange(): lax.all_to_all(values, axes, 0, 0, axis_index_groups=order, tiled=True)  53.5 us
    all_to_all x1, blocking collectives, exchange(): lax.all_to_all(values, axes, 0, 0, axis_index_groups=order, tiled=True)  17.7 us
    all_to_all x2, waiting for transfers between devices, exchange(): lax.all_to_all(values, axes, 0, 0, axis_index_groups=order, tiled=True)  13.5 us
    pallas_call x1, Pallas kernels, local(): pl.pallas_call(attention, out_shape=(near((heads * rows, HD), F32), near(...  2.27 us
  transfers between devices with their start and end apart: 2, of which 2 were waited for; matrix products, arithmetic and copies ran while one was open for 0% of the time, Pallas kernels for 3%

profile of v4, /device:TPU:1, one launch (start us, length us, event | category | flops | bytes accessed | tf_op | source)
XLA Modules:
  0.0 93.8 jit_solution(3297328833336595609)
XLA Ops:
  0.6 0.8 pad_maximum_fusion
  1.4 1.2 %broadcast_in_dim.15 = bf16[16,256,128]{2,1,0:T(8,128)(2,1)} broadcast(bf16[256,128]{1,0:T(8,128)(2,1)S(1)} %pad_maximum_fusion), dimensions={1,2} | broadcast | bytes 1114112 | tf_op jit(solution)/shard_map/broadcast_in_dim | solution.py:217
  2.6 0.0 copy-start
  2.6 0.0 copy-start.1
  2.6 0.0 copy-start.2
  2.6 0.0 copy-start.5
  2.6 0.0 copy-start.4
  2.6 0.0 copy-start.6
  2.6 9.8 %all-to-all-start = ((bf16[16,256,128]{2,1,0:T(8,128)(2,1)}), bf16[16,256,128]{2,1,0:T(8,128)(2,1)S(1)}, u32[]{:S(2)}, u32[]{:S(2)}) async-start(bf16[16,256,128]{2,1,0:T(8,128)(2,1)} %broadcast_in_dim.15), calls=%async_computation | async-start | bytes 2097152 | tf_op jit(solution)/shard_map/all_to_all | solution.py:202
  12.4 0.0 copy-done
  12.4 0.0 copy-done.1
  12.4 0.0 copy-done.2
  12.5 0.0 copy-done.5
  12.5 0.6 prologue.1
  13.1 7.1 %all-to-all-done.kv_ref = bf16[16,256,128]{2,1,0:T(8,128)(2,1)S(1)} async-done(((bf16[16,256,128]{2,1,0:T(8,128)(2,1)}), bf16[16,256,128]{2,1,0:T(8,128)(2,1)S(1)}, u32[]{:S(2)}, u32[]{:S(2)}) %all-to-all-start) | async-done | bytes 1048608 | tf_op jit(solution)/shard_map/all_to_all | solution.py:202
  20.2 0.0 copy-done.4
  20.2 0.0 copy-done.6
  20.2 2.3 %attention.1 = (f32[1024,128]{1,0:T(8,128)S(1)}, bf16[16,136,256]{2,1,0:T(8,128)(2,1)S(1)}) custom-call(s32[1]{0:T(128)} %bitcast.block_ref, bf16[16,256,128]{2,1,0:T(8,128)(2,1)S(1)} %all-to-all-done.kv_ref, bf16[1024,128]{1,0:T(8,128)(2,1)S(1)} %get-tuple-element.12.qn_ref, bf16[128,1024]{1,0:T(8,128)(2,1)S(1)} %get-tuple-element.13.qt_ref, ...), custom_call_target="tpu_custom_call" | custom-call | tf_op jit(solution)/shard_map/attention/pallas_call | solution.py:229
  22.5 17.7 %all_to_all.15.parts_ref = bf16[16,136,256]{2,1,0:T(8,128)(2,1)S(1)} all-to-all(bf16[16,136,256]{2,1,0:T(8,128)(2,1)S(1)} %get-tuple-element.17), channel_id=1, replica_groups={{896,960,0,64,128,192,256,320,384,448,512,576,640,704,768,832},{897,961..., dimensions={0} | all-to-all | bytes 2228224 | tf_op jit(solution)/shard_map/all_to_all | solution.py:202
  40.1 0.0 copy-start.3
  40.1 0.6 near_sum.1
  40.8 43.7 %all-to-all-start.2 = ((bf16[64,2,128]{2,1,0:T(2,128)(2,1)}), bf16[64,2,128]{2,1,0:T(2,128)(2,1)S(1)}, u32[]{:S(2)}, u32[]{:S(2)}) async-start(bf16[64,2,128]{2,1,0:T(2,128)(2,1)} %near_sum.1), calls=%async_computation.2 | async-start | bytes 65536 | tf_op jit(solution)/shard_map/all_to_all | solution.py:202
  84.5 1.4 %query_end.1 = f32[128,1024]{1,0:T(8,128)} custom-call(f32[1024,128]{1,0:T(8,128)S(1)} %get-tuple-element.16.dq_ref, bf16[128,1024]{1,0:T(8,128)(2,1)S(1)} %bitcast.14, f32[1,128]{1,0:T(1,128)S(1)} %bitcast.22), custom_call_target="tpu_custom_call" | custom-call | tf_op jit(solution)/shard_map/query_end/pallas_call | solution.py:243
  85.9 0.0 copy-done.3
  85.9 0.9 key_end.1
  86.7 6.5 %all-to-all-done.2.gains_ref = bf16[64,2,128]{2,1,0:T(2,128)(2,1)S(1)} async-done(((bf16[64,2,128]{2,1,0:T(2,128)(2,1)}), bf16[64,2,128]{2,1,0:T(2,128)(2,1)S(1)}, u32[]{:S(2)}, u32[]{:S(2)}) %all-to-all-start.2) | async-done | bytes 32800 | tf_op jit(solution)/shard_map/all_to_all | solution.py:202
  93.2 0.6 far_sum.1
Async XLA Ops:
  2.6 9.8 %copy-start = (bf16[1,128,1024]{2,1,0:T(8,128)(2,1)S(1)}, bf16[1,128,1024]{2,1,0:T(8,128)(2,1)}, u32[]{:S(2)}) copy-start(bf16[1,128,1024]{2,1,0:T(8,128)(2,1)} %param.8) | copy-start | bytes 786436
  2.6 9.9 %copy-start.1 = (bf16[1,128,1024]{2,1,0:T(8,128)(2,1)S(1)}, bf16[1,128,1024]{2,1,0:T(8,128)(2,1)}, u32[]{:S(2)}) copy-start(bf16[1,128,1024]{2,1,0:T(8,128)(2,1)} %param.12) | copy-start | bytes 786436
  2.6 9.9 %copy-start.2 = (bf16[1,128,1024]{2,1,0:T(8,128)(2,1)S(1)}, bf16[1,128,1024]{2,1,0:T(8,128)(2,1)}, u32[]{:S(2)}) copy-start(bf16[1,128,1024]{2,1,0:T(8,128)(2,1)} %param.11) | copy-start | bytes 786436
  2.6 9.9 %copy-start.5 = (f32[128]{0:T(128)S(1)}, f32[128]{0:T(128)}, u32[]{:S(2)}) copy-start(f32[128]{0:T(128)} %param.14) | copy-start | bytes 1540
  2.6 17.6 %copy-start.4 = (f32[1,8,128]{2,1,0:T(8,128)S(1)}, f32[1,8,128]{2,1,0:T(8,128)}, u32[]{:S(2)}) copy-start(f32[1,8,128]{2,1,0:T(8,128)} %param.13) | copy-start | bytes 12292
  2.6 17.6 %copy-start.6 = (f32[128]{0:T(128)S(1)}, f32[128]{0:T(128)}, u32[]{:S(2)}) copy-start(f32[128]{0:T(128)} %param.15) | copy-start | bytes 1540
  2.6 17.6 %all-to-all-start = ((bf16[16,256,128]{2,1,0:T(8,128)(2,1)}), bf16[16,256,128]{2,1,0:T(8,128)(2,1)S(1)}, u32[]{:S(2)}, u32[]{:S(2)}) async-start(bf16[16,256,128]{2,1,0:T(8,128)(2,1)} %broadcast_in_dim.15), calls=%async_computation | async-start | bytes 2097152 | tf_op jit(solution)/shard_map/all_to_all | solution.py:202
  40.1 45.7 %copy-start.3 = (bf16[1,128,128]{2,1,0:T(8,128)(2,1)S(1)}, bf16[1,128,128]{2,1,0:T(8,128)(2,1)}, u32[]{:S(2)}) copy-start(bf16[1,128,128]{2,1,0:T(8,128)(2,1)} %param.9) | copy-start | bytes 98308
  40.8 52.4 %all-to-all-start.2 = ((bf16[64,2,128]{2,1,0:T(2,128)(2,1)}), bf16[64,2,128]{2,1,0:T(2,128)(2,1)S(1)}, u32[]{:S(2)}, u32[]{:S(2)}) async-start(bf16[64,2,128]{2,1,0:T(2,128)(2,1)} %near_sum.1), calls=%async_computation.2 | async-start | bytes 65536 | tf_op jit(solution)/shard_map/all_to_all | solution.py:202
